TPU v7x, 32 devices: a whole 2x2x4 slice. The times are simulated.
32 devices in a mesh: rep: 4 (over x, core), shard: 8 (over z, y).
Axes of the slice: x: 2, y: 2, z: 4, core: 2. Of those that a mesh axis runs over, the one named last changes fastest.
Arguments:
- tokens: bfloat16 [4096, 2048], P(('rep', 'shard')), may hold values from -6 to 6
- segment_ids: int32 [4096], P(('rep', 'shard')), may hold values from 0 to 15, as said below
- positions: int32 [4096], P(('rep', 'shard')), may hold values from 0 to 127, as said below
- first_gain: float32 [2048], P('shard'), may hold values from 0.1 to 1.9
- first_shift: float32 [2048], P('shard'), may hold values from -1.75 to 1.75
- project_weight: bfloat16 [2048, 6144], P('shard'), may hold values from -0.125 to 0.125
- project_bias: float32 [6144], P('shard'), may hold values from -1.75 to 1.75
- mixing_weight: bfloat16 [2048, 2048], P('shard'), may hold values from -1 to 1
- mixing_bias: float32 [2048], P('shard'), may hold values from -1.75 to 1.75
- second_gain: float32 [2048], P('shard'), may hold values from 0.1 to 1.9
- second_shift: float32 [2048], P('shard'), may hold values from -1.75 to 1.75
- widen_weight: bfloat16 [2048, 8192], P('shard'), may hold values from -0.125 to 0.125
- widen_bias: float32 [8192], P('shard'), may hold values from -3 to 3
- narrow_weight: bfloat16 [8192, 2048], P('shard'), may hold values from -0.0625 to 0.0625
- narrow_bias: float32 [2048], P('shard'), may hold values from -1.75 to 1.75
- cotangent: bfloat16 [4096, 2048], P(('rep', 'shard')), may hold values from -6 to 6
Outputs:
- output: bfloat16 [4096, 2048], P(('rep', 'shard'))
- input_grad: bfloat16 [4096, 2048], P(('rep', 'shard'))
- first_gain_grad: float32 [2048], P('shard')
- first_shift_grad: float32 [2048], P('shard')
- project_weight_grad: float32 [2048, 6144], P('shard')
- project_bias_grad: float32 [6144], P('shard')
- mixing_weight_grad: float32 [2048, 2048], P('shard')
- mixing_bias_grad: float32 [2048], P('shard')
- second_gain_grad: float32 [2048], P('shard')
- second_shift_grad: float32 [2048], P('shard')
- widen_weight_grad: float32 [2048, 8192], P('shard')
- widen_bias_grad: float32 [8192], P('shard')
- narrow_weight_grad: float32 [8192, 2048], P('shard')
- narrow_bias_grad: float32 [2048], P('shard')
Inputs may be any that keep to these rules, and one draw needn't show every extreme that they name: `segment_ids`: documents never cross an aligned block of 128 tokens and begin only at positions within the block that are multiples of 8; in each block ids start at 0 and rise by one at each new document; some block holds 16 documents. `positions`: each token's position counts from 0 at the first token of its document; some block holds a single document.
All inputs are finite; a program needn't handle non-finite values.
Results may differ from a plain program's by a relative error of at most 0.015.
Values may be sent and summed in bfloat16 or wider, within the bound.
A program may use at most 640 MiB of HBM per device.

v0:
```python
import math

import jax
import jax.numpy as jnp
from jax import lax
from jax.experimental import pallas as pl
from jax.experimental.pallas import tpu as pltpu
from jax.sharding import PartitionSpec as P

D = 2048
HEADS = 8
HEAD_DIM = 256
ROT = 64
FF = 8192


def layer_norm(values, gain, shift):
    center = values - jnp.mean(values, axis=-1, keepdims=True)
    spread = jnp.mean(center * center, axis=-1, keepdims=True)
    return center * lax.rsqrt(spread + 1e-05) * gain + shift


def angles(positions):
    freqs = 10000.0 ** (-(jnp.arange(ROT // 2, dtype=jnp.float32) * 2.0 / ROT))
    turned = positions.astype(jnp.float32)[..., None] * freqs
    return (jnp.cos(turned), jnp.sin(turned))


def rotary(values, cosine, sine):
    half = ROT // 2
    front = values[..., :half]
    back = values[..., half:ROT]
    return jnp.concatenate(
        [front * cosine - back * sine, back * cosine + front * sine, values[..., ROT:]], axis=-1
    )


def exact_gelu(values):
    return jax.nn.gelu(values, approximate=False)


def contract_rows(left, right):
    return lax.dot_general(
        left, right, (((0,), (0,)), ((), ())), preferred_element_type=jnp.float32
    )


def times_rows(left, piece):
    return lax.dot_general(
        left, piece, (((1,), (1,)), ((), ())), preferred_element_type=jnp.float32
    )


def weight_terms(left_one, left_two, left_mix, left_act, d_joint, d_widened, cotangent):

    def wide_term(start, count):
        return jnp.concatenate(
            [
                contract_rows(left_one, d_joint),
                contract_rows(left_two, d_widened),
                contract_rows(left_mix, cotangent),
            ],
            axis=1,
        )

    def down_term(start, count):
        return contract_rows(left_act, cotangent)

    return (wide_term, down_term)


def per_device(
    tokens,
    segment_ids,
    positions,
    first_gain,
    first_shift,
    project_weight,
    project_bias,
    mixing_weight,
    mixing_bias,
    second_gain,
    second_shift,
    widen_weight,
    widen_bias,
    narrow_weight,
    narrow_bias,
    cotangent,
):
    length = tokens.shape[0]
    shards = lax.axis_size("shard")
    gain_one, shift_one, gain_two, shift_two, joint_bias, mix_bias, wide_bias, narrow_full = (
        lax.all_gather(first_gain, "shard", axis=0, tiled=True),
        lax.all_gather(first_shift, "shard", axis=0, tiled=True),
        lax.all_gather(second_gain, "shard", axis=0, tiled=True),
        lax.all_gather(second_shift, "shard", axis=0, tiled=True),
        lax.all_gather(project_bias, "shard", axis=0, tiled=True),
        lax.all_gather(mixing_bias, "shard", axis=0, tiled=True),
        lax.all_gather(widen_bias, "shard", axis=0, tiled=True),
        lax.all_gather(narrow_bias, "shard", axis=0, tiled=True),
    )
    inputs = tokens.astype(jnp.float32)
    first_norm, first_pull = jax.vjp(layer_norm, inputs, gain_one, shift_one)
    second_norm, second_pull = jax.vjp(layer_norm, inputs, gain_two, shift_two)
    first = first_norm.astype(jnp.bfloat16)
    second = second_norm.astype(jnp.bfloat16)
    pieces = (
        lax.all_gather(project_weight, "shard", axis=0, tiled=True),
        lax.all_gather(widen_weight, "shard", axis=0, tiled=True),
    )
    part_one = jnp.dot(first, pieces[0], preferred_element_type=jnp.float32)
    part_two = jnp.dot(second, pieces[1], preferred_element_type=jnp.float32)
    joint = part_one + joint_bias
    widened = part_two + wide_bias
    shaped = joint.reshape(length, 3, HEADS, HEAD_DIM)
    cosine, sine = angles(positions)
    cosine = cosine[:, None, :]
    sine = sine[:, None, :]

    def place(query_in, key_in):
        return (rotary(query_in, cosine, sine) * HEAD_DIM ** (-0.5), rotary(key_in, cosine, sine))

    (query_turned, key_turned), rotate_pull = jax.vjp(place, shaped[:, 0], shaped[:, 1])
    query = query_turned.astype(jnp.bfloat16)
    keys = key_turned.astype(jnp.bfloat16)
    values = shaped[:, 2].astype(jnp.bfloat16)
    order = jnp.arange(length)
    allowed = ((segment_ids[:, None] == segment_ids[None, :]) & (order[:, None] >= order[None, :]))[
        None
    ]

    def masked_scores():
        raw = jnp.einsum("qhe,khe->hqk", query, keys, preferred_element_type=jnp.float32)
        return jnp.where(allowed, raw, -1e30)

    scores = masked_scores()
    highest = jnp.max(scores, axis=-1, keepdims=True)
    raised = jnp.exp(scores - highest)
    summed = jnp.sum(raised, axis=-1, keepdims=True)
    log_summed = highest + jnp.log(summed)
    weights = (raised / summed).astype(jnp.bfloat16)
    context = (
        jnp.einsum("hqk,khe->qhe", weights, values, preferred_element_type=jnp.float32)
        .reshape(length, D)
        .astype(jnp.bfloat16)
    )
    attention = (
        jnp.dot(
            context,
            lax.all_gather(mixing_weight, "shard", axis=0, tiled=True),
            preferred_element_type=jnp.float32,
        )
        + mix_bias
    )
    active_full, gelu_pull = jax.vjp(exact_gelu, widened)
    active = active_full.astype(jnp.bfloat16)
    mlp = (
        jnp.dot(
            active,
            lax.all_gather(narrow_weight, "shard", axis=0, tiled=True),
            preferred_element_type=jnp.float32,
        )
        + narrow_full
    )
    output = (inputs + attention + mlp).astype(jnp.bfloat16)

    def back_rows(piece):
        return times_rows(cotangent, piece)

    d_active = back_rows(lax.all_gather(narrow_weight, "shard", axis=0, tiled=True))
    d_widened = gelu_pull(d_active)[0].astype(jnp.bfloat16)
    d_context = back_rows(lax.all_gather(mixing_weight, "shard", axis=0, tiled=True))
    d_context = d_context.astype(jnp.bfloat16).reshape(length, HEADS, HEAD_DIM)
    again = jnp.exp(masked_scores() - log_summed)
    again_low = again.astype(jnp.bfloat16)
    d_weights = jnp.einsum("qhe,khe->hqk", d_context, values, preferred_element_type=jnp.float32)
    d_values = jnp.einsum("hqk,qhe->khe", again_low, d_context, preferred_element_type=jnp.float32)
    d_scores = (again * (d_weights - jnp.sum(d_weights * again, axis=-1, keepdims=True))).astype(
        jnp.bfloat16
    )
    d_query = jnp.einsum("hqk,khe->qhe", d_scores, keys, preferred_element_type=jnp.float32)
    d_keys = jnp.einsum("hqk,qhe->khe", d_scores, query, preferred_element_type=jnp.float32)
    d_query_in, d_key_in = rotate_pull((d_query, d_keys))
    d_joint = jnp.concatenate(
        [d_query_in.reshape(length, D), d_key_in.reshape(length, D), d_values.reshape(length, D)],
        axis=1,
    ).astype(jnp.bfloat16)
    pieces = lax.all_gather((project_weight, widen_weight), "shard", axis=0, tiled=True)
    stacked = jnp.concatenate(
        [times_rows(d_joint, pieces[0]), times_rows(d_widened, pieces[1])], axis=0
    )
    d_in_one, d_gain_one, d_shift_one = first_pull(stacked[:length])
    d_in_two, d_gain_two, d_shift_two = second_pull(stacked[length:])
    input_grad = (cotangent.astype(jnp.float32) + d_in_one + d_in_two).astype(jnp.bfloat16)
    sums = lax.psum(
        (
            d_gain_one,
            d_shift_one,
            d_gain_two,
            d_shift_two,
            jnp.sum(d_joint, axis=0, dtype=jnp.float32),
            jnp.sum(cotangent, axis=0, dtype=jnp.float32),
            jnp.sum(d_widened, axis=0, dtype=jnp.float32),
        ),
        ("rep", "shard"),
    )
    owner = lax.axis_index("shard")

    def own_part(vector):
        share = vector.shape[0] // shards
        return lax.dynamic_slice_in_dim(vector, owner * share, share)

    owned = [own_part(vector) for vector in sums]
    wide_term, down_term = weight_terms(
        first, second, context, active, d_joint, d_widened, cotangent
    )
    wide_part = lax.psum_scatter(
        wide_term(jnp.int32(0), lax.axis_size("shard") * (D // shards)).astype(jnp.bfloat16),
        "shard",
        scatter_dimension=0,
        tiled=True,
    ).astype(jnp.float32)
    down_part = lax.psum_scatter(
        down_term(jnp.int32(0), lax.axis_size("shard") * (FF // shards)).astype(jnp.bfloat16),
        "shard",
        scatter_dimension=0,
        tiled=True,
    ).astype(jnp.float32)
    wide_part, down_part = (
        lax.psum(wide_part.astype(jnp.bfloat16), "rep").astype(jnp.float32),
        lax.psum(down_part.astype(jnp.bfloat16), "rep").astype(jnp.float32),
    )
    return (
        output,
        input_grad,
        owned[0],
        owned[1],
        wide_part[:, : 3 * D],
        owned[4],
        wide_part[:, 3 * D + FF :],
        owned[5],
        owned[2],
        owned[3],
        wide_part[:, 3 * D : 3 * D + FF],
        owned[6],
        down_part,
        owned[5],
    )


MESH = pl.DeviceIdType.MESH
ANY = pl.BlockSpec(memory_space=pl.ANY)


def places():
    rep, me = lax.axis_index("rep"), lax.axis_index("shard")
    core, side = rep % 2, rep // 2
    col, line = me % 2, me // 2
    return rep, me, core, side, col, line


def greet(peers):
    barrier = pltpu.get_barrier_semaphore()
    for peer in peers:
        pl.semaphore_signal(barrier, inc=1, device_id=peer, device_id_type=MESH)
    pl.semaphore_wait(barrier, len(peers))


def remote(source, target, send, recv, device):
    return pltpu.make_async_remote_copy(
        src_ref=source,
        dst_ref=target,
        send_sem=send,
        recv_sem=recv,
        device_id=device,
        device_id_type=MESH,
    )


F32, BF16 = jnp.float32, jnp.bfloat16
CHUNK = 256


def turned(value, cosine, sine):
    near = value[:, :128]
    lane = lax.broadcasted_iota(jnp.int32, near.shape, 1)
    partner = jnp.where(
        lane < ROT // 2,
        pltpu.roll(near, 128 - ROT // 2, 1),
        pltpu.roll(near, ROT // 2, 1),
    )
    return jnp.concatenate([near * cosine + partner * sine, value[:, 128:]], axis=1)


def dot(left, right, dims=((1,), (0,))):
    return lax.dot_general(left, right, (dims, ((), ())), preferred_element_type=F32)


def forward_kernel(
    tok, cot, wide_one, wide_two, mix, narrow,
    gain_one, shift_one, gain_two, shift_two, mix_bias, narrow_bias, joint_bias, wide_bias,
    segments, positions,
    cot_all, norm_out, cols_one_out, cols_two_out, first_out, second_out,
    query_out, key_out, value_out, probs_out, context_out, active_out, slope_out,
    out_part, cosine_out, sine_out, gains_out, bias_out,
    tok_all, cols_one, cols_two, mix_v, narrow_v, norms, first, second, joint, query, key, value,
    probs, context, active, slope, partial, cosines, sines, small, small_all, table,
    line_send, line_recv, col_send, col_recv,
    own_sem, piece_send, piece_recv, side_send, side_recv, core_send, core_recv,
    small_send, small_recv, load_sem, save_sem,
):
    rep, me, core, side, col, line = places()
    twin = rep + 1 - 2 * core
    across = rep + 2 - 4 * side
    twin_across = across + 1 - 2 * core
    other = me + 1 - 2 * col
    wide = cols_one.shape[1] // 3
    two_wide = cols_two.shape[1]
    rows = wide_one.shape[0]
    share = rows // 4
    length = tok.shape[0]
    width = tok.shape[1]

    offset = 0
    for ref in (gain_one, shift_one, gain_two, shift_two, mix_bias, narrow_bias, joint_bias,
                wide_bias, segments, positions):
        count = ref.shape[0]
        small[0:1, offset : offset + count] = ref[...].astype(F32)[None, :]
        offset += count

    greet(
        [(rep, (me + step) % 8) for step in range(1, 8)]
        + [(twin, me), (across, me)]
    )

    def along(which, array, gathered, direction, step):
        owner = line - direction * (step - 1)
        source = array if step == 1 else gathered.at[owner * 2 + col]
        lane = which * 6 + (0 if direction == 1 else 3) + step - 1
        return remote(
            source,
            gathered.at[owner * 2 + col],
            line_send.at[lane],
            line_recv.at[lane],
            (rep, (line + direction) * 2 + col),
        )

    def sends(direction, step):
        if direction == 1:
            return (line >= step - 1) & (line <= 2)
        return (line <= 4 - step) & (line >= 1)

    def gets(direction, step):
        if direction == 1:
            return line >= step
        return line <= 3 - step

    def sideways(which, array, gathered, direction, step):
        owner = line - direction * step
        source = array if step == 0 else gathered.at[owner * 2 + col]
        lane = which * 7 + (0 if direction == 1 else 3) + step
        return remote(
            source,
            gathered.at[owner * 2 + col],
            col_send.at[lane],
            col_recv.at[lane],
            (rep, other),
        )

    def from_other(which, gathered, direction, step):
        owner = line - direction * step
        lane = which * 7 + (0 if direction == 1 else 3) + step
        here = gathered.at[owner * 2 + 1 - col]
        return remote(here, here, col_send.at[lane], col_recv.at[lane], (rep, other))

    pairs = ((tok, tok_all), (cot, cot_all))
    turns = [(direction, step) for step in (1, 2, 3) for direction in (1, -1)]

    def begin(which):
        array, gathered = pairs[which]
        for direction in (1, -1):
            @pl.when(sends(direction, 1))
            def _(direction=direction):
                along(which, array, gathered, direction, 1).start()
        sideways(which, array, gathered, 1, 0).start()

    def pass_on(which, direction, step):
        array, gathered = pairs[which]

        @pl.when(gets(direction, step))
        def _():
            owner = line - direction * step
            lane = which * 6 + (0 if direction == 1 else 3) + step - 1
            here = gathered.at[owner * 2 + col]
            remote(
                here, here, line_send.at[lane], line_recv.at[lane], (rep, other)
            ).wait_recv()
            sideways(which, array, gathered, direction, step).start()

        if step < 3:
            @pl.when(sends(direction, step + 1))
            def _():
                along(which, array, gathered, direction, step + 1).start()

    def landed(which):
        gathered = pairs[which][1]
        for direction, step in turns:
            @pl.when(gets(direction, step))
            def _(direction=direction, step=step):
                from_other(which, gathered, direction, step).wait_recv()

        from_other(which, gathered, 1, 0).wait_recv()

    def sent(which):
        array, gathered = pairs[which]
        for direction, step in turns:
            @pl.when(sends(direction, step))
            def _(direction=direction, step=step):
                along(which, array, gathered, direction, step).wait_send()

            @pl.when(gets(direction, step))
            def _(direction=direction, step=step):
                sideways(which, array, gathered, direction, step).wait_send()

        sideways(which, array, gathered, 1, 0).wait_send()

    mine = pl.multiple_of(rep * share, share)

    def pieces(step):
        target = (me + step) % 8
        place = pl.ds(pl.multiple_of(me * rows + rep * share, share), share)
        out = []
        for part in range(3):
            out.append(
                remote(
                    wide_one.at[
                        pl.ds(mine, share),
                        pl.ds(pl.multiple_of((part * 8 + target) * wide, wide), wide),
                    ],
                    cols_one.at[place, pl.ds(part * wide, wide)],
                    piece_send.at[step - 1, part],
                    piece_recv.at[step - 1, part],
                    (rep, target),
                )
            )
        out.append(
            remote(
                wide_two.at[
                    pl.ds(mine, share),
                    pl.ds(pl.multiple_of(target * two_wide, two_wide), two_wide),
                ],
                cols_two.at[place, :],
                piece_send.at[step - 1, 3],
                piece_recv.at[step - 1, 3],
                (rep, target),
            )
        )
        return out

    def arrived(step):
        source = (me + 8 - step) % 8
        place = pl.ds(pl.multiple_of(source * rows + rep * share, share), share)
        here = [cols_one.at[place, pl.ds(part * wide, wide)] for part in range(3)]
        here.append(cols_two.at[place, :])
        return [
            remote(
                ref, ref, piece_send.at[step - 1, part], piece_recv.at[step - 1, part],
                (rep, source),
            )
            for part, ref in enumerate(here)
        ]

    def shares(step, quarter, send, recv, lane, device):
        source = (me + 8 - step) % 8
        place = pl.ds(pl.multiple_of(source * rows + quarter * share, share), share)
        return [
            remote(
                array.at[place, :], array.at[place, :],
                send.at[lane, step - 1, index], recv.at[lane, step - 1, index], device,
            )
            for index, array in enumerate((cols_one, cols_two))
        ]

    def little(step):
        return remote(
            small, small_all.at[me], small_send.at[step - 1], small_recv.at[step - 1],
            (rep, (me + step) % 8),
        )

    begin(0)
    for step in range(1, 8):
        little(step).start()
    for step in range(1, 8):
        for copy in pieces(step):
            copy.start()
    here = pl.ds(pl.multiple_of(me * rows, rows), rows)
    own = [
        pltpu.make_async_copy(tok, tok_all.at[me], own_sem.at[0]),
        pltpu.make_async_copy(cot, cot_all.at[me], own_sem.at[1]),
        pltpu.make_async_copy(small, small_all.at[me], own_sem.at[2]),
        pltpu.make_async_copy(
            wide_two.at[:, pl.ds(pl.multiple_of(me * two_wide, two_wide), two_wide)],
            cols_two.at[here, :],
            own_sem.at[3],
        ),
    ] + [
        pltpu.make_async_copy(
            wide_one.at[:, pl.ds(pl.multiple_of((part * 8 + me) * wide, wide), wide)],
            cols_one.at[here, pl.ds(part * wide, wide)],
            own_sem.at[4 + part],
        )
        for part in range(3)
    ]
    for copy in own:
        copy.start()
    loads = [
        pltpu.make_async_copy(mix, mix_v, load_sem.at[0]),
        pltpu.make_async_copy(narrow, narrow_v, load_sem.at[1]),
    ]
    for copy in loads:
        copy.start()
    for direction, step in turns:
        pass_on(0, direction, step)
    begin(1)
    for step in range(1, 8):
        source = (me + 8 - step) % 8
        remote(
            small_all.at[source], small_all.at[source], small_send.at[step - 1],
            small_recv.at[step - 1], (rep, source),
        ).wait_recv()
    own[0].wait()
    own[2].wait()
    for kind in range(6):
        for shard in range(8):
            table[kind : kind + 1, shard * 256 : shard * 256 + 256] = small_all[
                shard, :, kind * 256 : kind * 256 + 256
            ]
    for step in range(1, 8):
        for copy in arrived(step):
            copy.wait_recv()
        for copy in shares(step, rep, side_send, side_recv, 0, (across, me)):
            copy.start()
        for copy in shares(step, rep, core_send, core_recv, 0, (twin, me)):
            copy.start()
    landed(0)

    gains_one, shifts_one = table[0:1, :], table[1:2, :]
    gains_two, shifts_two = table[2:3, :], table[3:4, :]

    @pl.loop(0, 8 * length // 32)
    def _(index):
        block, part = index // (length // 32), index % (length // 32)
        at = pl.ds(pl.multiple_of(part * 32, 32), 32)
        raw = tok_all[block, at, :].astype(F32)
        center = raw - jnp.mean(raw, axis=-1, keepdims=True)
        spread = jnp.mean(center * center, axis=-1, keepdims=True)
        norm = center * lax.rsqrt(spread + 1e-05)
        there = pl.ds(pl.multiple_of(index * 32, 32), 32)
        norms[there, :] = norm.astype(BF16)
        first[there, :] = (norm * gains_one + shifts_one).astype(BF16)
        second[there, :] = (norm * gains_two + shifts_two).astype(BF16)

    saves = [
        pltpu.make_async_copy(norms, norm_out, save_sem.at[0]),
        pltpu.make_async_copy(first, first_out, save_sem.at[1]),
        pltpu.make_async_copy(second, second_out, save_sem.at[2]),
    ]
    for copy in saves:
        copy.start()

    for step in range(1, 8):
        for copy in shares(step, across, side_send, side_recv, 0, (across, me)):
            copy.wait_recv()
        for copy in shares(step, across, core_send, core_recv, 1, (twin, me)):
            copy.start()
    for step in range(1, 8):
        for copy in shares(step, twin, core_send, core_recv, 0, (twin, me)):
            copy.wait_recv()
    for step in range(1, 8):
        for copy in shares(step, twin_across, core_send, core_recv, 1, (twin, me)):
            copy.wait_recv()
    for copy in own[3:]:
        copy.wait()
    for copy in loads:
        copy.wait()
    late = [
        pltpu.make_async_copy(cols_one, cols_one_out, save_sem.at[3]),
        pltpu.make_async_copy(cols_two, cols_two_out, save_sem.at[4]),
    ]
    for copy in late:
        copy.start()
    saves += late

    for part in range(3):
        spot = part * 8 + me
        table[6:7, part * wide : (part + 1) * wide] = small_all[
            spot // 3, :, pl.ds(pl.multiple_of(1536 + (spot % 3) * 256, 256), 256)
        ]
    bias_row = table[6:7, 0 : 3 * wide]
    wide_row = small[0:1, 2304 : 2304 + two_wide]

    def project(start):
        at = pl.ds(start, CHUNK)
        for part in range(3):
            spot = slice(part * wide, (part + 1) * wide)
            joint[at, spot] = dot(first[at, :], cols_one[:, spot]) + bias_row[:, spot]
        for part in range(two_wide // 256):
            spot = slice(part * 256, (part + 1) * 256)
            value_now = dot(second[at, :], cols_two[:, spot]) + wide_row[:, spot]
            cdf = 0.5 * (1.0 + lax.erf(value_now * (0.5**0.5)))
            density = jnp.exp(-0.5 * value_now * value_now) * (0.5 / jnp.pi) ** 0.5
            active[at, spot] = (value_now * cdf).astype(BF16)
            slope[at, spot] = (cdf + value_now * density).astype(BF16)

    lane = lax.broadcasted_iota(jnp.int32, (1, 128), 1)
    frequency = jnp.where(
        lane < ROT,
        jnp.exp((lane % (ROT // 2)).astype(F32) * (-2.0 / ROT * math.log(10000.0))),
        0.0,
    )
    signs = jnp.where(lane < ROT // 2, -1.0, 1.0)
    tall = lax.broadcasted_iota(jnp.int32, (length, length), 0)
    flat = lax.broadcasted_iota(jnp.int32, (length, length), 1)
    ids_at = 2304 + two_wide

    def attend(block, start):
        at = pl.ds(start, length)
        ids = jnp.broadcast_to(small_all[block, :, ids_at : ids_at + 128], (length, length))
        spots = jnp.broadcast_to(
            small_all[block, :, ids_at + 128 : ids_at + 256], (length, length)
        )
        angle = spots.T * frequency
        cosine, sine = jnp.cos(angle), jnp.sin(angle) * signs
        query_now = (turned(joint[at, 0:wide], cosine, sine) * HEAD_DIM**-0.5).astype(BF16)
        key_now = turned(joint[at, wide : 2 * wide], cosine, sine).astype(BF16)
        value_now = joint[at, 2 * wide :].astype(BF16)
        scores = dot(query_now, key_now, ((1,), (1,)))
        allowed = (ids == ids.T) & (flat <= tall)
        scores = jnp.where(allowed, scores, -1e30)
        lifted = jnp.exp(scores - jnp.max(scores, axis=-1, keepdims=True))
        weights = lifted / jnp.sum(lifted, axis=-1, keepdims=True)
        cosines[at, :], sines[at, :] = cosine, sine
        query[at, :], key[at, :], value[at, :] = query_now, key_now, value_now
        probs[at, :] = weights
        context[at, :] = dot(weights.astype(BF16), value_now).astype(BF16)

    def finish(start):
        at = pl.ds(start, CHUNK)
        for part in range(width // 256):
            spot = slice(part * 256, (part + 1) * 256)
            partial[at, spot] = (
                dot(context[at, :], mix_v[:, spot]) + dot(active[at, :], narrow_v[:, spot])
            ).astype(BF16)

    pending = list(turns)
    for index in range(8 * length // CHUNK):
        project(index * CHUNK)
        for direction, step in pending[:1]:
            pass_on(1, direction, step)
        pending = pending[1:]
        for part in range(CHUNK // length):
            block = index * (CHUNK // length) + part
            attend(block, block * length)
        finish(index * CHUNK)
        for direction, step in pending[:1]:
            pass_on(1, direction, step)
        pending = pending[1:]
    for direction, step in pending:
        pass_on(1, direction, step)
    gains_out[...] = table[...]
    bias_out[...] = table[4:5, :] + table[5:6, :]
    late = [
        pltpu.make_async_copy(source, target, save_sem.at[5 + index])
        for index, (source, target) in enumerate(
            (
                (query, query_out), (key, key_out), (value, value_out), (probs, probs_out),
                (context, context_out), (active, active_out), (slope, slope_out),
                (partial, out_part), (cosines, cosine_out), (sines, sine_out),
            )
        )
    ]
    for copy in late:
        copy.start()
    saves += late

    sent(0)
    for step in range(1, 8):
        for copy in pieces(step):
            copy.wait_send()
        for copy in shares(step, rep, side_send, side_recv, 0, (across, me)):
            copy.wait_send()
        for copy in shares(step, rep, core_send, core_recv, 0, (twin, me)):
            copy.wait_send()
        for copy in shares(step, across, core_send, core_recv, 1, (twin, me)):
            copy.wait_send()
        little(step).wait_send()
    own[1].wait()
    for copy in saves:
        copy.wait()
    sent(1)
    landed(1)


def forward(tok, cot, wide_one, wide_two, mix, narrow, vectors):
    dma = pltpu.SemaphoreType.DMA
    length, width = tok.shape
    rows, one = wide_one.shape
    two = wide_two.shape[1]
    one, two = one // 8, two // 8
    total = 8 * length
    struct = jax.ShapeDtypeStruct
    vmem = pl.BlockSpec(memory_space=pltpu.VMEM)
    saved = [
        ((total, HEAD_DIM), BF16), ((total, HEAD_DIM), BF16), ((total, HEAD_DIM), BF16),
        ((total, length), F32), ((total, HEAD_DIM), BF16), ((total, two), BF16),
        ((total, two), BF16), ((total, width), BF16), ((total, length), F32),
        ((total, length), F32),
    ]
    packed = sum(v.shape[0] for v in vectors)
    return pl.pallas_call(
        forward_kernel,
        out_shape=(
            struct((8, length, width), BF16),
            struct((total, width), BF16),
            struct((rows * 8, one), BF16),
            struct((rows * 8, two), BF16),
            struct((total, width), BF16),
            struct((total, width), BF16),
        )
        + tuple(struct(*s) for s in saved)
        + (struct((8, width), F32), struct((1, width), F32)),
        in_specs=[ANY] * 6 + [vmem] * len(vectors),
        out_specs=(ANY,) * 16 + (vmem,) * 2,
        scratch_shapes=[
            pltpu.VMEM((8, length, width), BF16),
            pltpu.VMEM((rows * 8, one), BF16),
            pltpu.VMEM((rows * 8, two), BF16),
            pltpu.VMEM(mix.shape, BF16),
            pltpu.VMEM(narrow.shape, BF16),
            pltpu.VMEM((total, width), BF16),
            pltpu.VMEM((total, width), BF16),
            pltpu.VMEM((total, width), BF16),
            pltpu.VMEM((total, one), F32),
        ]
        + [pltpu.VMEM(*s) for s in saved]
        + [
            pltpu.VMEM((1, packed), F32),
            pltpu.VMEM((8, 1, packed), F32),
            pltpu.VMEM((8, width), F32),
            dma((12,)), dma((12,)), dma((14,)), dma((14,)),
            dma((7,)), dma((7, 4)), dma((7, 4)),
            dma((1, 7, 2)), dma((1, 7, 2)), dma((2, 7, 2)), dma((2, 7, 2)),
            dma((7,)), dma((7,)), dma((2,)), dma((15,)),
        ],
        compiler_params=pltpu.CompilerParams(
            collective_id=0, has_side_effects=True, vmem_limit_bytes=60 << 20
        ),
        name="forward",
    )(tok, cot, wide_one, wide_two, mix, narrow, *vectors)


def backward_kernel(
    cot_all, norm_all, first, second, cols_one, cols_two, mix, narrow,
    query_all, key_all, value_all, probs_all, context_all, active_all, slope_all,
    cosine_all, sine_all, out_part, table,
    out_sum, in_sum, one_full, two_full, mix_full, narrow_full, vec_full,
    grad_one, grad_two, grad_mix, grad_nar,
    core_one, core_two, core_mix, core_nar,
    side_one, side_two, side_mix, side_nar,
    cot, pair, duo, wide, d_widened, mix_v, query, key, value, probs, context, d_context,
    d_joint, cosine, sine, own_act, col_act, line_act, total, sums,
    vec, vec_got, vec_mid, vec_rep,
    load_sem, act_sem, cs, cr, ss, sr, ys, yr, zs, zr, ps, pr, fs, fr, vs, vr, us, ur, ds_sem,
):
    rep, me, core, side, col, line = places()
    twin = rep + 1 - 2 * core
    across = rep + 2 - 4 * side
    diagonal = across + 1 - 2 * core
    other = me + 1 - 2 * col
    length = out_sum.shape[0]
    width = out_sum.shape[1]
    tokens = wide.shape[0]
    half = width // 2
    two_wide = d_widened.shape[1]
    one_wide = d_joint.shape[1]
    part_wide = one_wide // 3
    share = grad_one.shape[2]
    greet(
        [(rep, (me + step) % 8) for step in range(1, 8)]
        + [(twin, me), (across, me), (diagonal, me)]
    )
    grads = (
        (grad_one, core_one, side_one),
        (grad_two, core_two, side_two),
        (grad_mix, core_mix, side_mix),
        (grad_nar, core_nar, side_nar),
    )

    def core_copy(index, slot):
        full, got, _ = grads[index]
        quarter = (across if slot == 0 else rep) + 1 - 2 * core
        return remote(
            full.at[quarter], got.at[slot], cs.at[index, slot], cr.at[index, slot],
            (twin, me),
        )

    def side_copy(index):
        full, _, got = grads[index]
        return remote(full.at[across], got, ss.at[index], sr.at[index], (across, me))

    def block_rows(target, column):
        return pl.ds(pl.multiple_of((target * 2 + column) * length, length), length)

    def col_copy(index, step):
        target = (line + step) % 4
        if index == 0:
            source = out_part.at[block_rows(target, 1 - col), :]
        else:
            source = wide.at[block_rows(target, 1 - col), :]
        return remote(
            source, col_act.at[index, step], ys.at[index, step], yr.at[index, step],
            (rep, other),
        )

    def own_block(index, step):
        if index == 0:
            return own_act.at[step]
        return wide.at[block_rows((line + step) % 4, col), :]

    def own_load(step):
        return pltpu.make_async_copy(
            out_part.at[block_rows((line + step) % 4, col), :], own_act.at[step],
            act_sem.at[step],
        )

    def line_copy(index, step):
        return remote(
            own_block(index, step), line_act.at[index, step - 1],
            zs.at[index, step - 1], zr.at[index, step - 1],
            (rep, ((line + step) % 4) * 2 + col),
        )

    def vec_copy(step):
        target = (me + step) % 8
        return remote(
            vec.at[target], vec_got.at[step - 1], vs.at[step - 1], vr.at[step - 1],
            (rep, target),
        )

    def vec_share(step):
        return remote(
            vec_mid, vec_rep.at[step - 1], us.at[step - 1], ur.at[step - 1],
            ((rep + step) % 4, me),
        )

    def load(source, target, lane):
        copy = pltpu.make_async_copy(source, target, load_sem.at[lane])
        copy.start()
        return copy

    active, slope = duo.at[pl.ds(0, tokens), :], duo.at[pl.ds(tokens, tokens), :]
    got_cot = load(cot_all, cot, 0)
    got_active = load(active_all, active, 1)
    got_context = load(context_all, context, 2)
    for step in (2, 1, 3, 0):
        col_copy(0, step).start()
    got_narrow = [
        load(narrow.at[:, pl.ds(0, half)], pair.at[pl.ds(0, two_wide), :], 3),
        load(narrow.at[:, pl.ds(half, half)], pair.at[pl.ds(two_wide, two_wide), :], 4),
    ]
    got_slope = load(slope_all, slope, 5)
    got_second = load(second, wide, 6)
    got_mix = load(mix, mix_v, 7)
    got_heads = [
        load(query_all, query, 8), load(key_all, key, 9), load(value_all, value, 10),
        load(probs_all, probs, 11), load(cosine_all, cosine, 12), load(sine_all, sine, 13),
    ]
    for step in range(4):
        own_load(step).start()
    vec[...] = jnp.zeros_like(vec)
    sums[...] = jnp.zeros_like(sums)

    def add_two(target, left, right):
        target[...] = (left[...].astype(F32) + right[...].astype(F32)).astype(BF16)

    def chunks(refs, function):
        shape = refs[0].shape
        if len(shape) == 3:
            per = shape[1] // 16

            @pl.loop(0, shape[0] * per)
            def _(index):
                at = pl.ds(pl.multiple_of((index % per) * 16, 16), 16)
                function(*[ref.at[index // per, at, :] for ref in refs])
        else:

            @pl.loop(0, shape[0] // 16)
            def _(index):
                at = pl.ds(pl.multiple_of(index * 16, 16), 16)
                function(*[ref.at[at, :] for ref in refs])

    def send_across(index):
        full, got, _ = grads[index]
        core_copy(index, 0).wait_recv()
        here = full.at[across]
        chunks((here, got.at[0]), lambda left, right: add_two(left, left, right))
        side_copy(index).start()

    got_active.wait()
    got_cot.wait()

    def narrow_quarter(quarter):
        at = pl.ds(pl.multiple_of(quarter * 256, 256), 256)
        for part in range(width // 512):
            spot = pl.ds(part * 512, 512)
            grad_nar[quarter, :, spot] = dot(
                active[:, at], cot[:, spot], ((0,), (0,))
            ).astype(BF16)

    @pl.loop(0, 2)
    def _(slot):
        narrow_quarter(jnp.where(slot == 0, diagonal, twin))

    core_copy(3, 0).start()
    core_copy(3, 1).start()

    @pl.loop(0, 2)
    def _(slot):
        narrow_quarter(jnp.where(slot == 0, across, rep))

    send_across(3)
    got_context.wait()
    for part in range(width // 512):
        spot = pl.ds(part * 512, 512)
        found = dot(context[...], cot[:, spot], ((0,), (0,))).astype(BF16)
        for quarter in range(4):
            grad_mix[quarter, :, spot] = found[quarter * share : (quarter + 1) * share]
    core_copy(2, 0).start()
    core_copy(2, 1).start()

    for copy in got_narrow:
        copy.wait()
    got_slope.wait()

    @pl.loop(0, tokens // 256)
    def _(index):
        at = pl.ds(pl.multiple_of(index * 256, 256), 256)
        for part in range(two_wide // 256):
            spot = pl.ds(part * 256, 256)
            low, high = pl.ds(part * 256, 256), pl.ds(two_wide + part * 256, 256)
            found = dot(cot[at, 0:half], pair[low, :], ((1,), (1,)))
            found = found + dot(cot[at, half:width], pair[high, :], ((1,), (1,)))
            found = (found * slope[at, spot].astype(F32)).astype(BF16)
            d_widened[at, spot] = found
            sums[5:6, spot] = sums[5:6, spot] + jnp.sum(
                found.astype(F32), axis=0, keepdims=True
            )

    got_cols = [load(cols_two, pair, 3)]
    send_across(2)
    got_second.wait()

    @pl.loop(0, 8)
    def _(shard):
        at = pl.ds(pl.multiple_of(shard * 256, 256), 256)
        for part in range(two_wide // 512):
            spot = pl.ds(part * 512, 512)
            found = dot(wide[:, at], d_widened[:, spot], ((0,), (0,))).astype(BF16)
            for quarter in range(4):
                grad_two[quarter, shard, :, spot] = found[
                    quarter * share : (quarter + 1) * share
                ]

    core_copy(1, 0).start()
    core_copy(1, 1).start()
    got_first = load(first, wide, 6)
    got_cols.append(load(cols_one, duo.at[:, pl.ds(0, one_wide)], 1))

    got_mix.wait()
    for copy in got_heads:
        copy.wait()

    @pl.loop(0, tokens // 256)
    def _(index):
        at = pl.ds(pl.multiple_of(index * 256, 256), 256)
        d_context[at, :] = dot(cot[at, :], mix_v[...], ((1,), (1,))).astype(BF16)

    @pl.loop(0, length // 16)
    def _(index):
        at = pl.ds(pl.multiple_of(me * length + index * 16, 16), 16)
        sums[4:5, :] = sums[4:5, :] + jnp.sum(
            cot[at, :].astype(F32), axis=0, keepdims=True
        )

    got_norm = load(norm_all, cot, 0)
    send_across(1)

    @pl.loop(0, 8)
    def _(block):
        at = pl.ds(pl.multiple_of(block * length, length), length)
        weights = probs[at, :]
        pull = d_context[at, :]
        d_weights = dot(pull, value[at, :], ((1,), (1,)))
        d_value = dot(weights.astype(BF16), pull, ((0,), (0,)))
        inner = jnp.sum(d_weights * weights, axis=-1, keepdims=True)
        d_scores = (weights * (d_weights - inner)).astype(BF16)
        d_query = dot(d_scores, key[at, :])
        d_key = dot(d_scores, query[at, :], ((0,), (0,)))
        turn_by, back = cosine[at, :], -sine[at, :]
        pieces = (
            turned(d_query, turn_by, back) * HEAD_DIM**-0.5,
            turned(d_key, turn_by, back),
            d_value,
        )
        for part, piece in enumerate(pieces):
            low = piece.astype(BF16)
            spot = slice(part * part_wide, (part + 1) * part_wide)
            d_joint[at, spot] = low
            sums[6:7, spot] = sums[6:7, spot] + jnp.sum(
                low.astype(F32), axis=0, keepdims=True
            )

    got_first.wait()

    @pl.loop(0, 8)
    def _(shard):
        at = pl.ds(pl.multiple_of(shard * 256, 256), 256)
        for part in range(3):
            spot = pl.ds(part * part_wide, part_wide)
            found = dot(wide[:, at], d_joint[:, spot], ((0,), (0,))).astype(BF16)
            for quarter in range(4):
                grad_one[quarter, shard, :, spot] = found[
                    quarter * share : (quarter + 1) * share
                ]

    core_copy(0, 0).start()
    core_copy(0, 1).start()
    send_across(0)

    def send_along(index, step):
        col_copy(index, step).wait_recv()
        if index == 0:
            own_load(step).wait()
        chunks(
            (own_block(index, step), col_act.at[index, step]),
            lambda left, right: add_two(left, left, right),
        )
        line_copy(index, step).start()

    for step in (2, 1, 3):
        send_along(0, step)

    for copy in got_cols:
        copy.wait()
    got_norm.wait()

    for step in (2, 1, 3, 0):
        start = ((line + step) % 4) * 2 * length

        @pl.loop(0, width // 256)
        def _(index, start=start):
            at = pl.ds(pl.multiple_of(start, 2 * length), 2 * length)
            spot = pl.ds(pl.multiple_of(index * 256, 256), 256)
            d_one = dot(d_joint[at, :], duo[spot, 0:one_wide], ((1,), (1,)))
            d_two = dot(d_widened[at, :], pair[spot, :], ((1,), (1,)))
            now = cot[at, spot].astype(F32)
            rows = (d_one * now, d_one, d_two * now, d_two)
            for place, piece in enumerate(rows):
                sums[place : place + 1, spot] = sums[place : place + 1, spot] + jnp.sum(
                    piece, axis=0, keepdims=True
                )
            wide[at, spot] = (d_one * table[0:1, spot] + d_two * table[2:3, spot]).astype(
                BF16
            )

        col_copy(1, step).start()

    for shard in range(8):
        for place in range(5):
            start = place * 256 if place < 4 else 1792
            vec[shard, :, start : start + 256] = sums[
                place : place + 1, shard * 256 : (shard + 1) * 256
            ]
    vec[me, :, 2048:3072] = sums[5:6, 0:two_wide]
    for part in range(3):
        place = part * 8 + me
        start = pl.multiple_of(1024 + (place % 3) * 256, 256)
        vec[place // 3, :, pl.ds(start, 256)] = sums[
            6:7, part * part_wide : (part + 1) * part_wide
        ]
    for step in range(1, 8):
        vec_copy(step).start()

    my_rows = pl.ds(pl.multiple_of(rep * share, share), share)

    def whole(index):
        full, got, arrived = grads[index]
        core_copy(index, 1).wait_recv()
        side_copy(index).wait_recv()

        def add(left, right, far):
            left[...] = (
                left[...].astype(F32) + right[...].astype(F32) + far[...].astype(F32)
            ).astype(BF16)

        chunks((full.at[rep], got.at[1], arrived), add)

    def pieces(index, step, source_shard, target_shard):
        local = grads[index][0].at[rep, target_shard]
        if index == 1:
            at = pl.ds(pl.multiple_of(source_shard * two_wide, two_wide), two_wide)
            return [
                remote(
                    local, two_full.at[my_rows, at], ps.at[step, 3], pr.at[step, 3],
                    (rep, target_shard),
                )
            ]
        out = []
        for part in range(3):
            start = pl.multiple_of((part * 8 + source_shard) * part_wide, part_wide)
            out.append(
                remote(
                    local.at[:, pl.ds(part * part_wide, part_wide)],
                    one_full.at[my_rows, pl.ds(start, part_wide)],
                    ps.at[step, part], pr.at[step, part], (rep, target_shard),
                )
            )
        return out

    def own_pieces(index):
        local = grads[index][0].at[rep, me]
        if index == 1:
            at = pl.ds(pl.multiple_of(me * two_wide, two_wide), two_wide)
            return [pltpu.make_async_copy(local, two_full.at[my_rows, at], ds_sem.at[3])]
        out = []
        for part in range(3):
            start = pl.multiple_of((part * 8 + me) * part_wide, part_wide)
            out.append(
                pltpu.make_async_copy(
                    local.at[:, pl.ds(part * part_wide, part_wide)],
                    one_full.at[my_rows, pl.ds(start, part_wide)],
                    ds_sem.at[part],
                )
            )
        return out

    for index in (1, 0):
        whole(index)
        for step in range(1, 8):
            for copy in pieces(index, step, me, (me + step) % 8):
                copy.start()
        for copy in own_pieces(index):
            copy.start()

    fulls = (one_full, two_full, mix_full, narrow_full)

    def spot_of(index, quarter):
        count = fulls[index].shape[0] // 4
        return fulls[index].at[pl.ds(pl.multiple_of(quarter * count, count), count), :]

    def hand(index, lane, source, quarter, device):
        return remote(
            source, spot_of(index, quarter), fs.at[index, lane], fr.at[index, lane], device
        )

    own_full = []
    for index in (3, 2):
        whole(index)
        source = grads[index][0].at[rep]
        hand(index, 0, source, rep, (across, me)).start()
        hand(index, 1, source, rep, (twin, me)).start()
        copy = pltpu.make_async_copy(source, spot_of(index, rep), ds_sem.at[2 + index])
        copy.start()
        own_full.append(copy)

    for step in (2, 1, 3):
        send_along(1, step)

    for step in range(1, 8):
        vec_copy(step).wait_recv()
    running = vec[me]
    for step in range(1, 8):
        running = running + vec_got[step - 1]
    vec_mid[...] = running
    for step in range(1, 4):
        vec_share(step).start()

    for index in (1, 0):
        for copy in own_pieces(index):
            copy.wait()
        for step in range(1, 8):
            for copy in pieces(index, step, (me + 8 - step) % 8, me):
                copy.wait_recv()
        hand(index, 0, spot_of(index, rep), rep, (across, me)).start()
        hand(index, 1, spot_of(index, rep), rep, (twin, me)).start()

    for index in (0, 1):
        col_copy(index, 0).wait_recv()
        if index == 0:
            own_load(0).wait()
        for step in range(1, 4):
            line_copy(index, step).wait_recv()
        base = own_block(index, 0)

        @pl.loop(0, length // 16)
        def _(place, index=index, base=base):
            at = pl.ds(pl.multiple_of(place * 16, 16), 16)
            found = base[at, :].astype(F32) + col_act[index, 0, at, :].astype(F32)
            for step in range(3):
                found = found + line_act[index, step, at, :].astype(F32)
            total[at, :] = found

        copy = pltpu.make_async_copy(total, (out_sum, in_sum)[index], ds_sem.at[6])
        copy.start()
        copy.wait()

    for step in range(1, 4):
        vec_share(step).wait_recv()
    vec_full[...] = vec_mid[...] + vec_rep[0] + vec_rep[1] + vec_rep[2]

    for index in (3, 2, 1, 0):
        hand(index, 0, spot_of(index, across), across, (across, me)).wait_recv()
        hand(index, 2, spot_of(index, across), across, (twin, me)).start()
    for index in range(4):
        source = grads[index][0].at[rep] if index > 1 else spot_of(index, rep)
        hand(index, 0, source, rep, (across, me)).wait_send()
        hand(index, 1, source, rep, (twin, me)).wait_send()
        hand(index, 1, spot_of(index, twin), twin, (twin, me)).wait_recv()
        hand(index, 2, spot_of(index, across), across, (twin, me)).wait_send()
        hand(index, 2, spot_of(index, diagonal), diagonal, (twin, me)).wait_recv()
        side_copy(index).wait_send()
        for slot in (0, 1):
            core_copy(index, slot).wait_send()
    for index in (0, 1):
        for step in range(1, 8):
            for copy in pieces(index, step, me, (me + step) % 8):
                copy.wait_send()
        for step in range(4):
            col_copy(index, step).wait_send()
            if step:
                line_copy(index, step).wait_send()
    for step in range(1, 8):
        vec_copy(step).wait_send()
    for step in range(1, 4):
        vec_share(step).wait_send()
    for copy in own_full:
        copy.wait()


def backward(
    cot_all, norm, first, second, cols_one, cols_two, mix, narrow,
    heads, context, active, slope, cosine, sine, out_part, table,
):
    dma = pltpu.SemaphoreType.DMA
    struct = jax.ShapeDtypeStruct
    vmem = pl.BlockSpec(memory_space=pltpu.VMEM)
    tokens, width = cot_all.shape
    length = tokens // 8
    one, two = cols_one.shape[1], cols_two.shape[1]
    share = width // 32
    quarters = [
        (8, share, one), (8, share, two), (mix.shape[0] // 4, width),
        (narrow.shape[0] // 4, width),
    ]
    lanes = 4 * width // 8 + one + width // 8 + two
    return pl.pallas_call(
        backward_kernel,
        out_shape=(
            struct((length, width), F32),
            struct((length, width), F32),
            struct((4 * share, 8 * one), BF16),
            struct((4 * share, 8 * two), BF16),
            struct(mix.shape, BF16),
            struct(narrow.shape, BF16),
            struct((1, lanes), F32),
        ),
        in_specs=[ANY] * 18 + [vmem],
        out_specs=(ANY,) * 6 + (vmem,),
        scratch_shapes=[pltpu.VMEM((4,) + q, BF16) for q in quarters]
        + [pltpu.VMEM((2,) + q, BF16) for q in quarters]
        + [pltpu.VMEM(q, BF16) for q in quarters]
        + [
            pltpu.VMEM((tokens, width), BF16),
            pltpu.VMEM((width, two), BF16),
            pltpu.VMEM((2 * tokens, two), BF16),
            pltpu.VMEM((tokens, width), BF16),
            pltpu.VMEM((tokens, two), BF16),
            pltpu.VMEM(mix.shape, BF16),
        ]
        + [pltpu.VMEM(h.shape, h.dtype) for h in heads]
        + [
            pltpu.VMEM(context.shape, BF16),
            pltpu.VMEM(context.shape, BF16),
            pltpu.VMEM((tokens, one), BF16),
            pltpu.VMEM(cosine.shape, F32),
            pltpu.VMEM(sine.shape, F32),
            pltpu.VMEM((4, length, width), BF16),
            pltpu.VMEM((2, 4, length, width), BF16),
            pltpu.VMEM((2, 3, length, width), BF16),
            pltpu.VMEM((length, width), F32),
            pltpu.VMEM((8, width), F32),
            pltpu.VMEM((8, 1, lanes), F32),
            pltpu.VMEM((7, 1, lanes), F32),
            pltpu.VMEM((1, lanes), F32),
            pltpu.VMEM((3, 1, lanes), F32),
            dma((14,)), dma((4,)),
            dma((4, 2)), dma((4, 2)), dma((4,)), dma((4,)),
            dma((2, 4)), dma((2, 4)), dma((2, 3)), dma((2, 3)),
            dma((8, 4)), dma((8, 4)), dma((4, 3)), dma((4, 3)),
            dma((7,)), dma((7,)), dma((3,)), dma((3,)), dma((7,)),
        ],
        compiler_params=pltpu.CompilerParams(
            collective_id=1, has_side_effects=True, vmem_limit_bytes=60 << 20
        ),
        name="backward",
    )(
        cot_all, norm, first, second, cols_one, cols_two, mix, narrow,
        *heads, context, active, slope, cosine, sine, out_part, table,
    )


def tensor_parallel(
    tokens,
    segment_ids,
    positions,
    first_gain,
    first_shift,
    project_weight,
    project_bias,
    mixing_weight,
    mixing_bias,
    second_gain,
    second_shift,
    widen_weight,
    widen_bias,
    narrow_weight,
    narrow_bias,
    cotangent,
):
    (
        cot_all, norm, cols_one, cols_two, first, second, query, keys, values, probs,
        context, active, slope, out_part, cosine, sine, table, out_bias,
    ) = forward(
        tokens, cotangent, project_weight, widen_weight, mixing_weight, narrow_weight,
        (
            first_gain, first_shift, second_gain, second_shift, mixing_bias, narrow_bias,
            project_bias, widen_bias, segment_ids, positions,
        ),
    )
    out_sum, in_sum, full_one, full_two, full_mix, full_narrow, sums = backward(
        cot_all.reshape(-1, D), norm, first, second, cols_one, cols_two, mixing_weight,
        narrow_weight, (query, keys, values, probs), context, active, slope, cosine, sine,
        out_part, table,
    )
    own = tokens.astype(F32)
    own_center = own - jnp.mean(own, axis=-1, keepdims=True)
    own_scale = lax.rsqrt(
        jnp.mean(own_center * own_center, axis=-1, keepdims=True) + 1e-05
    )
    own_norm = own_center * own_scale
    output = (own + out_sum + out_bias).astype(BF16)
    pulled = own_scale * (
        in_sum
        - jnp.mean(in_sum, axis=-1, keepdims=True)
        - own_norm * jnp.mean(in_sum * own_norm, axis=-1, keepdims=True)
    )
    input_grad = (cotangent.astype(F32) + pulled).astype(BF16)
    flat = sums.reshape(-1)
    return (
        output,
        input_grad,
        flat[:256],
        flat[256:512],
        full_one.astype(F32),
        flat[1024:1792],
        full_mix.astype(F32),
        flat[1792:2048],
        flat[512:768],
        flat[768:1024],
        full_two.astype(F32),
        flat[2048:3072],
        full_narrow.astype(F32),
        flat[1792:2048],
    )


def solution(mesh):
    head_per_shard = mesh.shape["shard"] == HEADS and mesh.shape["rep"] == 4
    chosen = tensor_parallel if head_per_shard else per_device
    in_specs = (
        P(("rep", "shard"), None),
        P(("rep", "shard")),
        P(("rep", "shard")),
        P("shard"),
        P("shard"),
        P("shard", None),
        P("shard"),
        P("shard", None),
        P("shard"),
        P("shard"),
        P("shard"),
        P("shard", None),
        P("shard"),
        P("shard", None),
        P("shard"),
        P(("rep", "shard"), None),
    )
    out_specs = (
        P(("rep", "shard"), None),
        P(("rep", "shard"), None),
        P("shard"),
        P("shard"),
        P("shard", None),
        P("shard"),
        P("shard", None),
        P("shard"),
        P("shard"),
        P("shard"),
        P("shard", None),
        P("shard"),
        P("shard", None),
        P("shard"),
    )
    return jax.shard_map(
        chosen, mesh=mesh, in_specs=in_specs, out_specs=out_specs, check_vma=False
    )
```

profile of v0, /device:TPU:29, one launch (start us, length us, event | category | flops | bytes accessed | tf_op | source)
XLA Modules:
  0.0 370.2 jit_solution(247151525696199705)
XLA Ops:
  0.6 157.8 %forward.1 = (bf16[8,128,2048]{2,1,0:T(8,128)(2,1)}, bf16[1024,2048]{1,0:T(8,128)(2,1)}, bf16[2048,768]{1,0:T(8,128)(2,1)}, bf16[2048,1024]{1,0:T(8,128)(2,1)}, ...) custom-call(bf16[128,2048]{1,0:T(8,128)(2,1)} %tok.1, ...), custom_call_target="tpu_custom_call" | custom-call | tf_op jit(solution)/shard_map/forward/pallas_call | solution.py:720
  158.5 190.7 %backward.1 = (f32[128,2048]{1,0:T(8,128)}, f32[128,2048]{1,0:T(8,128)}, bf16[256,6144]{1,0:T(8,128)(2,1)}, bf16[256,8192]{1,0:T(8,128)(2,1)}, bf16[256,2048]{1,...) custom-call(bf16[1024,2048]{1,0:T(8,128)(2,1)} %bitcast.8, ...), custom_call_target="tpu_custom_call" | custom-call | tf_op jit(solution)/shard_map/backward/pallas_call | solution.py:1266
  349.1 0.0 copy-start.1
  349.2 6.7 %convert_element_type.30 = f32[256,8192]{1,0:T(8,128)} convert(bf16[256,8192]{1,0:T(8,128)(2,1)} %get-tuple-element.62) | non-fusion elementwise | flops 2097152 | bytes 12582912 | tf_op jit(solution)/shard_map/convert_element_type | solution.py:1380
  355.9 0.0 copy-done.1
  355.9 0.0 copy-start.3
  355.9 4.4 %convert_element_type.31 = f32[1024,2048]{1,0:T(8,128)} convert(bf16[1024,2048]{1,0:T(8,128)(2,1)S(1)} %copy-done.1) | non-fusion elementwise | flops 2097152 | bytes 12582912 | tf_op jit(solution)/shard_map/convert_element_type | solution.py:1382
  360.3 0.0 copy-done.3
  360.3 0.0 copy-start.5
  360.3 0.0 copy-start
  360.3 3.4 convert_element_type.28
  363.8 0.0 copy-start.2
  363.8 0.0 copy-start.4
  363.8 0.0 copy-start.6
  363.8 0.0 copy-start.8
  363.8 0.0 copy-done.5
  363.8 1.6 convert_element_type.29
  365.4 0.0 copy-start.7
  365.4 0.0 copy-done
  365.4 0.2 convert_reduce_fusion
  365.5 0.3 fusion.9
  365.8 0.0 copy-done.2
  365.8 0.3 fusion.12
  366.2 0.0 copy-done.4
  366.2 0.0 copy-done.6
  366.2 0.0 copy-done.8
  366.2 1.6 fusion.8
  367.8 0.0 copy-done.7
  367.8 0.6 fusion.13
  368.4 0.0 copy-start.9
  368.4 0.6 slice.55
  369.0 0.6 slice_reduce_fusion
  369.6 0.6 copy.31
  370.2 0.0 copy-done.9
  (3 shorter events, 0.0 us)
Async XLA Ops:
  349.1 6.7 %copy-start.1 = (bf16[1024,2048]{1,0:T(8,128)(2,1)S(1)}, bf16[1024,2048]{1,0:T(8,128)(2,1)}, u32[]{:S(2)}) copy-start(bf16[1024,2048]{1,0:T(8,128)(2,1)} %get-tuple-element.63) | copy-start | bytes 12582916
  355.9 4.5 %copy-start.3 = (bf16[256,6144]{1,0:T(8,128)(2,1)S(1)}, bf16[256,6144]{1,0:T(8,128)(2,1)}, u32[]{:S(2)}) copy-start(bf16[256,6144]{1,0:T(8,128)(2,1)} %get-tuple-element.60) | copy-start | bytes 9437188
  360.3 3.5 copy-start.5
  360.3 5.0 %copy-start = (bf16[128,2048]{1,0:T(8,128)(2,1)S(1)}, bf16[128,2048]{1,0:T(8,128)(2,1)}, u32[]{:S(2)}) copy-start(bf16[128,2048]{1,0:T(8,128)(2,1)} %tok.1) | copy-start | bytes 1572868
  363.8 2.1 copy-start.2
  363.8 2.4 copy-start.4
  363.8 2.5 copy-start.6
  363.8 2.5 copy-start.8
  365.4 2.5 copy-start.7
  368.4 1.8 copy-start.9
where the time goes:
time: 371 us; the launch traced here: 370 us
  Pallas kernels  348 us (94%)
  other arithmetic  18.6 us (5%)
    pallas_call x1, Pallas kernels, backward(): pl.pallas_call(backward_kernel, out_shape=(struct((length, width), F32),...  191 us
    pallas_call x1, Pallas kernels, forward(): pl.pallas_call(forward_kernel, out_shape=(struct((8, length, width), BF16...  158 us

commit v1 on v0

--- a/solution.py
+++ b/solution.py
@@ -487,12 +487,6 @@
             (rep, (me + step) % 8),
         )
 
-    begin(0)
-    for step in range(1, 8):
-        little(step).start()
-    for step in range(1, 8):
-        for copy in pieces(step):
-            copy.start()
     here = pl.ds(pl.multiple_of(me * rows, rows), rows)
     own = [
         pltpu.make_async_copy(tok, tok_all.at[me], own_sem.at[0]),
@@ -511,96 +505,105 @@
         )
         for part in range(3)
     ]
-    for copy in own:
-        copy.start()
     loads = [
         pltpu.make_async_copy(mix, mix_v, load_sem.at[0]),
         pltpu.make_async_copy(narrow, narrow_v, load_sem.at[1]),
     ]
-    for copy in loads:
-        copy.start()
-    for direction, step in turns:
-        pass_on(0, direction, step)
-    begin(1)
-    for step in range(1, 8):
-        source = (me + 8 - step) % 8
-        remote(
-            small_all.at[source], small_all.at[source], small_send.at[step - 1],
-            small_recv.at[step - 1], (rep, source),
-        ).wait_recv()
-    own[0].wait()
-    own[2].wait()
-    for kind in range(6):
-        for shard in range(8):
-            table[kind : kind + 1, shard * 256 : shard * 256 + 256] = small_all[
-                shard, :, kind * 256 : kind * 256 + 256
+
+    def send_small():
+        for step in range(1, 8):
+            little(step).start()
+
+    def send_pieces(*steps):
+        for step in steps:
+            for copy in pieces(step):
+                copy.start()
+
+    def load_own():
+        for copy in own + loads:
+            copy.start()
+
+    def take_small():
+        for step in range(1, 8):
+            source = (me + 8 - step) % 8
+            remote(
+                small_all.at[source], small_all.at[source], small_send.at[step - 1],
+                small_recv.at[step - 1], (rep, source),
+            ).wait_recv()
+        own[2].wait()
+        for kind in range(6):
+            for shard in range(8):
+                table[kind : kind + 1, shard * 256 : shard * 256 + 256] = small_all[
+                    shard, :, kind * 256 : kind * 256 + 256
+                ]
+        for part in range(3):
+            spot = part * 8 + me
+            table[6:7, part * wide : (part + 1) * wide] = small_all[
+                spot // 3, :, pl.ds(pl.multiple_of(1536 + (spot % 3) * 256, 256), 256)
             ]
-    for step in range(1, 8):
-        for copy in arrived(step):
-            copy.wait_recv()
-        for copy in shares(step, rep, side_send, side_recv, 0, (across, me)):
+        gains_out[...] = table[...]
+        bias_out[...] = table[4:5, :] + table[5:6, :]
+
+    def relay(*steps):
+        for step in steps:
+            for copy in arrived(step):
+                copy.wait_recv()
+            for copy in shares(step, rep, side_send, side_recv, 0, (across, me)):
+                copy.start()
+            for copy in shares(step, rep, core_send, core_recv, 0, (twin, me)):
+                copy.start()
+
+    def relay_across(*steps):
+        for step in steps:
+            for copy in shares(step, across, side_send, side_recv, 0, (across, me)):
+                copy.wait_recv()
+            for copy in shares(step, across, core_send, core_recv, 1, (twin, me)):
+                copy.start()
+
+    def take_weights():
+        for step in range(1, 8):
+            for copy in shares(step, twin, core_send, core_recv, 0, (twin, me)):
+                copy.wait_recv()
+        for step in range(1, 8):
+            for copy in shares(step, twin_across, core_send, core_recv, 1, (twin, me)):
+                copy.wait_recv()
+        for copy in own[3:]:
+            copy.wait()
+        for copy in loads:
+            copy.wait()
+        save((cols_one, cols_one_out), (cols_two, cols_two_out))
+
+    saves = []
+
+    def save(*items):
+        for source, target in items:
+            copy = pltpu.make_async_copy(source, target, save_sem.at[len(saves)])
             copy.start()
-        for copy in shares(step, rep, core_send, core_recv, 0, (twin, me)):
-            copy.start()
-    landed(0)
-
-    gains_one, shifts_one = table[0:1, :], table[1:2, :]
-    gains_two, shifts_two = table[2:3, :], table[3:4, :]
-
-    @pl.loop(0, 8 * length // 32)
-    def _(index):
-        block, part = index // (length // 32), index % (length // 32)
-        at = pl.ds(pl.multiple_of(part * 32, 32), 32)
-        raw = tok_all[block, at, :].astype(F32)
-        center = raw - jnp.mean(raw, axis=-1, keepdims=True)
-        spread = jnp.mean(center * center, axis=-1, keepdims=True)
-        norm = center * lax.rsqrt(spread + 1e-05)
-        there = pl.ds(pl.multiple_of(index * 32, 32), 32)
-        norms[there, :] = norm.astype(BF16)
-        first[there, :] = (norm * gains_one + shifts_one).astype(BF16)
-        second[there, :] = (norm * gains_two + shifts_two).astype(BF16)
-
-    saves = [
-        pltpu.make_async_copy(norms, norm_out, save_sem.at[0]),
-        pltpu.make_async_copy(first, first_out, save_sem.at[1]),
-        pltpu.make_async_copy(second, second_out, save_sem.at[2]),
-    ]
-    for copy in saves:
-        copy.start()
-
-    for step in range(1, 8):
-        for copy in shares(step, across, side_send, side_recv, 0, (across, me)):
-            copy.wait_recv()
-        for copy in shares(step, across, core_send, core_recv, 1, (twin, me)):
-            copy.start()
-    for step in range(1, 8):
-        for copy in shares(step, twin, core_send, core_recv, 0, (twin, me)):
-            copy.wait_recv()
-    for step in range(1, 8):
-        for copy in shares(step, twin_across, core_send, core_recv, 1, (twin, me)):
-            copy.wait_recv()
-    for copy in own[3:]:
-        copy.wait()
-    for copy in loads:
-        copy.wait()
-    late = [
-        pltpu.make_async_copy(cols_one, cols_one_out, save_sem.at[3]),
-        pltpu.make_async_copy(cols_two, cols_two_out, save_sem.at[4]),
-    ]
-    for copy in late:
-        copy.start()
-    saves += late
-
-    for part in range(3):
-        spot = part * 8 + me
-        table[6:7, part * wide : (part + 1) * wide] = small_all[
-            spot // 3, :, pl.ds(pl.multiple_of(1536 + (spot % 3) * 256, 256), 256)
-        ]
-    bias_row = table[6:7, 0 : 3 * wide]
-    wide_row = small[0:1, 2304 : 2304 + two_wide]
-
-    def project(start):
-        at = pl.ds(start, CHUNK)
+            saves.append(copy)
+
+    def norm_all():
+        gains_one, shifts_one = table[0:1, :], table[1:2, :]
+        gains_two, shifts_two = table[2:3, :], table[3:4, :]
+
+        @pl.loop(0, 8 * length // 32)
+        def _(index):
+            block, part = index // (length // 32), index % (length // 32)
+            at = pl.ds(pl.multiple_of(part * 32, 32), 32)
+            raw = tok_all[block, at, :].astype(F32)
+            center = raw - jnp.mean(raw, axis=-1, keepdims=True)
+            spread = jnp.mean(center * center, axis=-1, keepdims=True)
+            norm = center * lax.rsqrt(spread + 1e-05)
+            there = pl.ds(pl.multiple_of(index * 32, 32), 32)
+            norms[there, :] = norm.astype(BF16)
+            first[there, :] = (norm * gains_one + shifts_one).astype(BF16)
+            second[there, :] = (norm * gains_two + shifts_two).astype(BF16)
+
+        save((norms, norm_out), (first, first_out), (second, second_out))
+
+    def project(index):
+        bias_row = table[6:7, 0 : 3 * wide]
+        wide_row = small[0:1, 2304 : 2304 + two_wide]
+        at = pl.ds(index * CHUNK, CHUNK)
         for part in range(3):
             spot = slice(part * wide, (part + 1) * wide)
             joint[at, spot] = dot(first[at, :], cols_one[:, spot]) + bias_row[:, spot]
@@ -623,8 +626,8 @@
     flat = lax.broadcasted_iota(jnp.int32, (length, length), 1)
     ids_at = 2304 + two_wide
 
-    def attend(block, start):
-        at = pl.ds(start, length)
+    def attend(block):
+        at = pl.ds(block * length, length)
         ids = jnp.broadcast_to(small_all[block, :, ids_at : ids_at + 128], (length, length))
         spots = jnp.broadcast_to(
             small_all[block, :, ids_at + 128 : ids_at + 256], (length, length)
@@ -644,45 +647,65 @@
         probs[at, :] = weights
         context[at, :] = dot(weights.astype(BF16), value_now).astype(BF16)
 
-    def finish(start):
-        at = pl.ds(start, CHUNK)
+    def finish(index):
+        at = pl.ds(index * CHUNK, CHUNK)
         for part in range(width // 256):
             spot = slice(part * 256, (part + 1) * 256)
             partial[at, spot] = (
                 dot(context[at, :], mix_v[:, spot]) + dot(active[at, :], narrow_v[:, spot])
             ).astype(BF16)
 
-    pending = list(turns)
-    for index in range(8 * length // CHUNK):
-        project(index * CHUNK)
-        for direction, step in pending[:1]:
-            pass_on(1, direction, step)
-        pending = pending[1:]
-        for part in range(CHUNK // length):
-            block = index * (CHUNK // length) + part
-            attend(block, block * length)
-        finish(index * CHUNK)
-        for direction, step in pending[:1]:
-            pass_on(1, direction, step)
-        pending = pending[1:]
-    for direction, step in pending:
-        pass_on(1, direction, step)
-    gains_out[...] = table[...]
-    bias_out[...] = table[4:5, :] + table[5:6, :]
-    late = [
-        pltpu.make_async_copy(source, target, save_sem.at[5 + index])
-        for index, (source, target) in enumerate(
-            (
-                (query, query_out), (key, key_out), (value, value_out), (probs, probs_out),
-                (context, context_out), (active, active_out), (slope, slope_out),
-                (partial, out_part), (cosines, cosine_out), (sines, sine_out),
-            )
-        )
-    ]
-    for copy in late:
-        copy.start()
-    saves += late
-
+    def save_all():
+        save(
+            (query, query_out), (key, key_out), (value, value_out), (probs, probs_out),
+            (context, context_out), (active, active_out), (slope, slope_out),
+            (partial, out_part), (cosines, cosine_out), (sines, sine_out),
+        )
+
+    begin(0)
+    send_small()
+    load_own()
+    pass_on(0, 1, 1)
+    pass_on(0, -1, 1)
+    send_pieces(1,7,2,6)
+    pass_on(0, 1, 2)
+    pass_on(0, -1, 2)
+    send_pieces(3,5,4)
+    pass_on(0, 1, 3)
+    pass_on(0, -1, 3)
+    relay(1,7)
+    begin(1)
+    take_small()
+    own[0].wait()
+    relay(2,6)
+    landed(0)
+    norm_all()
+    relay(3,5,4)
+    pass_on(1, 1, 1)
+    pass_on(1, -1, 1)
+    relay_across(1,7,2,6,3,5,4)
+    pass_on(1, 1, 2)
+    pass_on(1, -1, 2)
+    take_weights()
+    project(0)
+    pass_on(1, 1, 3)
+    pass_on(1, -1, 3)
+    attend(0)
+    attend(1)
+    finish(0)
+    project(1)
+    attend(2)
+    attend(3)
+    finish(1)
+    project(2)
+    attend(4)
+    attend(5)
+    finish(2)
+    project(3)
+    attend(6)
+    attend(7)
+    finish(3)
+    save_all()
     sent(0)
     for step in range(1, 8):
         for copy in pieces(step):
@@ -808,11 +831,22 @@
         full, _, got = grads[index]
         return remote(full.at[across], got, ss.at[index], sr.at[index], (across, me))
 
+    inner = (line == 1) | (line == 2)
+
+    def target_of(step):
+        if step == 0:
+            return 3 * ((line + 1) % 2)
+        if step == 1:
+            return (line + 2) % 4
+        if step == 2:
+            return 1 + line % 2
+        return line
+
     def block_rows(target, column):
         return pl.ds(pl.multiple_of((target * 2 + column) * length, length), length)
 
     def col_copy(index, step):
-        target = (line + step) % 4
+        target = target_of(step)
         if index == 0:
             source = out_part.at[block_rows(target, 1 - col), :]
         else:
@@ -825,20 +859,25 @@
     def own_block(index, step):
         if index == 0:
             return own_act.at[step]
-        return wide.at[block_rows((line + step) % 4, col), :]
+        return wide.at[block_rows(target_of(step), col), :]
 
     def own_load(step):
         return pltpu.make_async_copy(
-            out_part.at[block_rows((line + step) % 4, col), :], own_act.at[step],
+            out_part.at[block_rows(target_of(step), col), :], own_act.at[step],
             act_sem.at[step],
         )
 
     def line_copy(index, step):
+        slot = jnp.where(inner, (2, 3, 3)[step], step)
+        goal = jnp.where(inner, target_of(step), 1 + line // 2)
         return remote(
-            own_block(index, step), line_act.at[index, step - 1],
-            zs.at[index, step - 1], zr.at[index, step - 1],
-            (rep, ((line + step) % 4) * 2 + col),
-        )
+            own_block(index, step), line_act.at[index, slot], zs.at[index, step],
+            zr.at[index, slot], (rep, goal * 2 + col),
+        )
+
+    def came(index, slot):
+        here = line_act.at[index, slot]
+        return here, remote(here, here, zs.at[index, 0], zr.at[index, slot], (rep, other))
 
     def vec_copy(step):
         target = (me + step) % 8
@@ -862,7 +901,7 @@
     got_cot = load(cot_all, cot, 0)
     got_active = load(active_all, active, 1)
     got_context = load(context_all, context, 2)
-    for step in (2, 1, 3, 0):
+    for step in range(4):
         col_copy(0, step).start()
     got_narrow = [
         load(narrow.at[:, pl.ds(0, half)], pair.at[pl.ds(0, two_wide), :], 3),
@@ -899,17 +938,22 @@
                 at = pl.ds(pl.multiple_of(index * 16, 16), 16)
                 function(*[ref.at[at, :] for ref in refs])
 
-    def send_across(index):
+    def across_sum(index):
         full, got, _ = grads[index]
         core_copy(index, 0).wait_recv()
         here = full.at[across]
         chunks((here, got.at[0]), lambda left, right: add_two(left, left, right))
         side_copy(index).start()
 
-    got_active.wait()
-    got_cot.wait()
-
-    def narrow_quarter(quarter):
+    def trade(index, slot):
+        core_copy(index, slot).start()
+
+    def wait(*copies):
+        for copy in copies:
+            copy.wait()
+
+    def narrow_grad(order):
+        quarter = (diagonal, twin, across, rep)[order]
         at = pl.ds(pl.multiple_of(quarter * 256, 256), 256)
         for part in range(width // 512):
             spot = pl.ds(part * 512, 512)
@@ -917,145 +961,113 @@
                 active[:, at], cot[:, spot], ((0,), (0,))
             ).astype(BF16)
 
-    @pl.loop(0, 2)
-    def _(slot):
-        narrow_quarter(jnp.where(slot == 0, diagonal, twin))
-
-    core_copy(3, 0).start()
-    core_copy(3, 1).start()
-
-    @pl.loop(0, 2)
-    def _(slot):
-        narrow_quarter(jnp.where(slot == 0, across, rep))
-
-    send_across(3)
-    got_context.wait()
-    for part in range(width // 512):
-        spot = pl.ds(part * 512, 512)
-        found = dot(context[...], cot[:, spot], ((0,), (0,))).astype(BF16)
-        for quarter in range(4):
-            grad_mix[quarter, :, spot] = found[quarter * share : (quarter + 1) * share]
-    core_copy(2, 0).start()
-    core_copy(2, 1).start()
-
-    for copy in got_narrow:
-        copy.wait()
-    got_slope.wait()
-
-    @pl.loop(0, tokens // 256)
-    def _(index):
-        at = pl.ds(pl.multiple_of(index * 256, 256), 256)
-        for part in range(two_wide // 256):
-            spot = pl.ds(part * 256, 256)
-            low, high = pl.ds(part * 256, 256), pl.ds(two_wide + part * 256, 256)
-            found = dot(cot[at, 0:half], pair[low, :], ((1,), (1,)))
-            found = found + dot(cot[at, half:width], pair[high, :], ((1,), (1,)))
-            found = (found * slope[at, spot].astype(F32)).astype(BF16)
-            d_widened[at, spot] = found
-            sums[5:6, spot] = sums[5:6, spot] + jnp.sum(
-                found.astype(F32), axis=0, keepdims=True
+    def mix_grad():
+        for part in range(width // 512):
+            spot = pl.ds(part * 512, 512)
+            found = dot(context[...], cot[:, spot], ((0,), (0,))).astype(BF16)
+            for quarter in range(4):
+                grad_mix[quarter, :, spot] = found[quarter * share : (quarter + 1) * share]
+
+    def through_gelu(low_index, high_index):
+        @pl.loop(low_index, high_index)
+        def _(index):
+            at = pl.ds(pl.multiple_of(index * 256, 256), 256)
+            for part in range(two_wide // 256):
+                spot = pl.ds(part * 256, 256)
+                low, high = pl.ds(part * 256, 256), pl.ds(two_wide + part * 256, 256)
+                found = dot(cot[at, 0:half], pair[low, :], ((1,), (1,)))
+                found = found + dot(cot[at, half:width], pair[high, :], ((1,), (1,)))
+                found = (found * slope[at, spot].astype(F32)).astype(BF16)
+                d_widened[at, spot] = found
+                sums[5:6, spot] = sums[5:6, spot] + jnp.sum(
+                    found.astype(F32), axis=0, keepdims=True
+                )
+
+    def wide_grad(low_index, high_index):
+        @pl.loop(low_index, high_index)
+        def _(shard):
+            at = pl.ds(pl.multiple_of(shard * 256, 256), 256)
+            for part in range(two_wide // 512):
+                spot = pl.ds(part * 512, 512)
+                found = dot(wide[:, at], d_widened[:, spot], ((0,), (0,))).astype(BF16)
+                for quarter in range(4):
+                    grad_two[quarter, shard, :, spot] = found[
+                        quarter * share : (quarter + 1) * share
+                    ]
+
+    def through_mix():
+        @pl.loop(0, tokens // 256)
+        def _(index):
+            at = pl.ds(pl.multiple_of(index * 256, 256), 256)
+            d_context[at, :] = dot(cot[at, :], mix_v[...], ((1,), (1,))).astype(BF16)
+
+        @pl.loop(0, length // 16)
+        def _(index):
+            at = pl.ds(pl.multiple_of(me * length + index * 16, 16), 16)
+            sums[4:5, :] = sums[4:5, :] + jnp.sum(
+                cot[at, :].astype(F32), axis=0, keepdims=True
             )
 
-    got_cols = [load(cols_two, pair, 3)]
-    send_across(2)
-    got_second.wait()
-
-    @pl.loop(0, 8)
-    def _(shard):
-        at = pl.ds(pl.multiple_of(shard * 256, 256), 256)
-        for part in range(two_wide // 512):
-            spot = pl.ds(part * 512, 512)
-            found = dot(wide[:, at], d_widened[:, spot], ((0,), (0,))).astype(BF16)
-            for quarter in range(4):
-                grad_two[quarter, shard, :, spot] = found[
-                    quarter * share : (quarter + 1) * share
-                ]
-
-    core_copy(1, 0).start()
-    core_copy(1, 1).start()
-    got_first = load(first, wide, 6)
-    got_cols.append(load(cols_one, duo.at[:, pl.ds(0, one_wide)], 1))
-
-    got_mix.wait()
-    for copy in got_heads:
-        copy.wait()
-
-    @pl.loop(0, tokens // 256)
-    def _(index):
-        at = pl.ds(pl.multiple_of(index * 256, 256), 256)
-        d_context[at, :] = dot(cot[at, :], mix_v[...], ((1,), (1,))).astype(BF16)
-
-    @pl.loop(0, length // 16)
-    def _(index):
-        at = pl.ds(pl.multiple_of(me * length + index * 16, 16), 16)
-        sums[4:5, :] = sums[4:5, :] + jnp.sum(
-            cot[at, :].astype(F32), axis=0, keepdims=True
-        )
-
-    got_norm = load(norm_all, cot, 0)
-    send_across(1)
-
-    @pl.loop(0, 8)
-    def _(block):
-        at = pl.ds(pl.multiple_of(block * length, length), length)
-        weights = probs[at, :]
-        pull = d_context[at, :]
-        d_weights = dot(pull, value[at, :], ((1,), (1,)))
-        d_value = dot(weights.astype(BF16), pull, ((0,), (0,)))
-        inner = jnp.sum(d_weights * weights, axis=-1, keepdims=True)
-        d_scores = (weights * (d_weights - inner)).astype(BF16)
-        d_query = dot(d_scores, key[at, :])
-        d_key = dot(d_scores, query[at, :], ((0,), (0,)))
-        turn_by, back = cosine[at, :], -sine[at, :]
-        pieces = (
-            turned(d_query, turn_by, back) * HEAD_DIM**-0.5,
-            turned(d_key, turn_by, back),
-            d_value,
-        )
-        for part, piece in enumerate(pieces):
-            low = piece.astype(BF16)
-            spot = slice(part * part_wide, (part + 1) * part_wide)
-            d_joint[at, spot] = low
-            sums[6:7, spot] = sums[6:7, spot] + jnp.sum(
-                low.astype(F32), axis=0, keepdims=True
+    def attend_back(low_index, high_index):
+        @pl.loop(low_index, high_index)
+        def _(block):
+            at = pl.ds(pl.multiple_of(block * length, length), length)
+            weights = probs[at, :]
+            pull = d_context[at, :]
+            d_weights = dot(pull, value[at, :], ((1,), (1,)))
+            d_value = dot(weights.astype(BF16), pull, ((0,), (0,)))
+            inner = jnp.sum(d_weights * weights, axis=-1, keepdims=True)
+            d_scores = (weights * (d_weights - inner)).astype(BF16)
+            d_query = dot(d_scores, key[at, :])
+            d_key = dot(d_scores, query[at, :], ((0,), (0,)))
+            turn_by, back = cosine[at, :], -sine[at, :]
+            pieces = (
+                turned(d_query, turn_by, back) * HEAD_DIM**-0.5,
+                turned(d_key, turn_by, back),
+                d_value,
             )
-
-    got_first.wait()
-
-    @pl.loop(0, 8)
-    def _(shard):
-        at = pl.ds(pl.multiple_of(shard * 256, 256), 256)
-        for part in range(3):
-            spot = pl.ds(part * part_wide, part_wide)
-            found = dot(wide[:, at], d_joint[:, spot], ((0,), (0,))).astype(BF16)
-            for quarter in range(4):
-                grad_one[quarter, shard, :, spot] = found[
-                    quarter * share : (quarter + 1) * share
-                ]
-
-    core_copy(0, 0).start()
-    core_copy(0, 1).start()
-    send_across(0)
+            for part, piece in enumerate(pieces):
+                low = piece.astype(BF16)
+                spot = slice(part * part_wide, (part + 1) * part_wide)
+                d_joint[at, spot] = low
+                sums[6:7, spot] = sums[6:7, spot] + jnp.sum(
+                    low.astype(F32), axis=0, keepdims=True
+                )
+
+    def project_grad(low_index, high_index):
+        @pl.loop(low_index, high_index)
+        def _(shard):
+            at = pl.ds(pl.multiple_of(shard * 256, 256), 256)
+            for part in range(3):
+                spot = pl.ds(part * part_wide, part_wide)
+                found = dot(wide[:, at], d_joint[:, spot], ((0,), (0,))).astype(BF16)
+                for quarter in range(4):
+                    grad_one[quarter, shard, :, spot] = found[
+                        quarter * share : (quarter + 1) * share
+                    ]
 
     def send_along(index, step):
         col_copy(index, step).wait_recv()
         if index == 0:
             own_load(step).wait()
-        chunks(
-            (own_block(index, step), col_act.at[index, step]),
-            lambda left, right: add_two(left, left, right),
-        )
+        here = own_block(index, step)
+
+        def add(left, right):
+            chunks((left, right), lambda one, two: add_two(one, one, two))
+
+        add(here, col_act.at[index, step])
+
+        if step > 0:
+            @pl.when(inner)
+            def _():
+                there, copy = came(index, step - 1)
+                copy.wait_recv()
+                add(here, there)
+
         line_copy(index, step).start()
 
-    for step in (2, 1, 3):
-        send_along(0, step)
-
-    for copy in got_cols:
-        copy.wait()
-    got_norm.wait()
-
-    for step in (2, 1, 3, 0):
-        start = ((line + step) % 4) * 2 * length
+    def input_part(step):
+        start = target_of(step) * 2 * length
 
         @pl.loop(0, width // 256)
         def _(index, start=start):
@@ -1075,21 +1087,22 @@
 
         col_copy(1, step).start()
 
-    for shard in range(8):
-        for place in range(5):
-            start = place * 256 if place < 4 else 1792
-            vec[shard, :, start : start + 256] = sums[
-                place : place + 1, shard * 256 : (shard + 1) * 256
+    def send_sums():
+        for shard in range(8):
+            for place in range(5):
+                start = place * 256 if place < 4 else 1792
+                vec[shard, :, start : start + 256] = sums[
+                    place : place + 1, shard * 256 : (shard + 1) * 256
+                ]
+        vec[me, :, 2048:3072] = sums[5:6, 0:two_wide]
+        for part in range(3):
+            place = part * 8 + me
+            start = pl.multiple_of(1024 + (place % 3) * 256, 256)
+            vec[place // 3, :, pl.ds(start, 256)] = sums[
+                6:7, part * part_wide : (part + 1) * part_wide
             ]
-    vec[me, :, 2048:3072] = sums[5:6, 0:two_wide]
-    for part in range(3):
-        place = part * 8 + me
-        start = pl.multiple_of(1024 + (place % 3) * 256, 256)
-        vec[place // 3, :, pl.ds(start, 256)] = sums[
-            6:7, part * part_wide : (part + 1) * part_wide
-        ]
-    for step in range(1, 8):
-        vec_copy(step).start()
+        for step in range(1, 8):
+            vec_copy(step).start()
 
     my_rows = pl.ds(pl.multiple_of(rep * share, share), share)
 
@@ -1144,28 +1157,27 @@
             )
         return out
 
-    for index in (1, 0):
-        whole(index)
-        for step in range(1, 8):
+    fulls = (one_full, two_full, mix_full, narrow_full)
+
+    def spot_of(index, quarter):
+        count = fulls[index].shape[0] // 4
+        return fulls[index].at[pl.ds(pl.multiple_of(quarter * count, count), count), :]
+
+    def hand(index, lane, source, quarter, device):
+        return remote(
+            source, spot_of(index, quarter), fs.at[index, lane], fr.at[index, lane], device
+        )
+
+    own_full = []
+
+    def scatter(index, *steps):
+        for step in steps:
             for copy in pieces(index, step, me, (me + step) % 8):
                 copy.start()
         for copy in own_pieces(index):
             copy.start()
 
-    fulls = (one_full, two_full, mix_full, narrow_full)
-
-    def spot_of(index, quarter):
-        count = fulls[index].shape[0] // 4
-        return fulls[index].at[pl.ds(pl.multiple_of(quarter * count, count), count), :]
-
-    def hand(index, lane, source, quarter, device):
-        return remote(
-            source, spot_of(index, quarter), fs.at[index, lane], fr.at[index, lane], device
-        )
-
-    own_full = []
-    for index in (3, 2):
-        whole(index)
+    def hand_out(index):
         source = grads[index][0].at[rep]
         hand(index, 0, source, rep, (across, me)).start()
         hand(index, 1, source, rep, (twin, me)).start()
@@ -1173,19 +1185,17 @@
         copy.start()
         own_full.append(copy)
 
-    for step in (2, 1, 3):
-        send_along(1, step)
-
-    for step in range(1, 8):
-        vec_copy(step).wait_recv()
-    running = vec[me]
-    for step in range(1, 8):
-        running = running + vec_got[step - 1]
-    vec_mid[...] = running
-    for step in range(1, 4):
-        vec_share(step).start()
-
-    for index in (1, 0):
+    def share_sums():
+        for step in range(1, 8):
+            vec_copy(step).wait_recv()
+        running = vec[me]
+        for step in range(1, 8):
+            running = running + vec_got[step - 1]
+        vec_mid[...] = running
+        for step in range(1, 4):
+            vec_share(step).start()
+
+    def hand_on(index):
         for copy in own_pieces(index):
             copy.wait()
         for step in range(1, 8):
@@ -1194,33 +1204,99 @@
         hand(index, 0, spot_of(index, rep), rep, (across, me)).start()
         hand(index, 1, spot_of(index, rep), rep, (twin, me)).start()
 
-    for index in (0, 1):
-        col_copy(index, 0).wait_recv()
+    def end_sum(index):
+        col_copy(index, 3).wait_recv()
         if index == 0:
-            own_load(0).wait()
-        for step in range(1, 4):
-            line_copy(index, step).wait_recv()
-        base = own_block(index, 0)
-
-        @pl.loop(0, length // 16)
-        def _(place, index=index, base=base):
-            at = pl.ds(pl.multiple_of(place * 16, 16), 16)
-            found = base[at, :].astype(F32) + col_act[index, 0, at, :].astype(F32)
-            for step in range(3):
-                found = found + line_act[index, step, at, :].astype(F32)
-            total[at, :] = found
-
+            own_load(3).wait()
+        here = own_block(index, 3)
+
+        def add(left, right):
+            left[...] = left[...] + right[...].astype(F32)
+
+        def begin(left, right, both):
+            both[...] = left[...].astype(F32) + right[...].astype(F32)
+
+        chunks((here, col_act.at[index, 3], total), begin)
+
+        for slot in (2, 3):
+            there, copy = came(index, slot)
+            copy.wait_recv()
+            chunks((total, there), add)
         copy = pltpu.make_async_copy(total, (out_sum, in_sum)[index], ds_sem.at[6])
         copy.start()
         copy.wait()
 
-    for step in range(1, 4):
-        vec_share(step).wait_recv()
-    vec_full[...] = vec_mid[...] + vec_rep[0] + vec_rep[1] + vec_rep[2]
-
-    for index in (3, 2, 1, 0):
+    def end_vec():
+        for step in range(1, 4):
+            vec_share(step).wait_recv()
+        vec_full[...] = vec_mid[...] + vec_rep[0] + vec_rep[1] + vec_rep[2]
+
+    def hand_twin(index):
         hand(index, 0, spot_of(index, across), across, (across, me)).wait_recv()
         hand(index, 2, spot_of(index, across), across, (twin, me)).start()
+
+    wait(got_active, got_cot)
+    narrow_grad(0)
+    trade(3, 0)
+    narrow_grad(1)
+    trade(3, 1)
+    narrow_grad(2)
+    across_sum(3)
+    narrow_grad(3)
+    wait(got_context)
+    mix_grad()
+    trade(2, 0)
+    trade(2, 1)
+    wait(*got_narrow, got_slope)
+    through_gelu(0, 4)
+    got_cols = [load(cols_two, pair, 3)]
+    across_sum(2)
+    wait(got_second)
+    send_along(0, 0)
+    wide_grad(0, 8)
+    trade(1, 0)
+    trade(1, 1)
+    got_first = load(first, wide, 6)
+    got_cols.append(load(cols_one, duo.at[:, pl.ds(0, one_wide)], 1))
+    wait(got_mix, *got_heads)
+    through_mix()
+    got_norm = load(norm_all, cot, 0)
+    across_sum(1)
+    send_along(0, 1)
+    attend_back(0, 8)
+    wait(got_first)
+    project_grad(0, 8)
+    trade(0, 0)
+    trade(0, 1)
+    across_sum(0)
+    wait(*got_cols, got_norm)
+    send_along(0, 2)
+    input_part(0)
+    input_part(1)
+    input_part(2)
+    input_part(3)
+    send_sums()
+    whole(1)
+    scatter(1, 1,7,2,6,3,5,4)
+    send_along(1, 0)
+    whole(0)
+    scatter(0, 1,7,2,6,3,5,4)
+    whole(3)
+    hand_out(3)
+    whole(2)
+    hand_out(2)
+    send_along(1, 1)
+    end_sum(0)
+    hand_on(1)
+    send_along(1, 2)
+    share_sums()
+    hand_on(0)
+    end_sum(1)
+    end_vec()
+    hand_twin(3)
+    hand_twin(2)
+    hand_twin(1)
+    hand_twin(0)
     for index in range(4):
         source = grads[index][0].at[rep] if index > 1 else spot_of(index, rep)
         hand(index, 0, source, rep, (across, me)).wait_send()
@@ -1237,7 +1313,7 @@
                 copy.wait_send()
         for step in range(4):
             col_copy(index, step).wait_send()
-            if step:
+            if step < 3:
                 line_copy(index, step).wait_send()
     for step in range(1, 8):
         vec_copy(step).wait_send()
@@ -1296,7 +1372,7 @@
             pltpu.VMEM(sine.shape, F32),
             pltpu.VMEM((4, length, width), BF16),
             pltpu.VMEM((2, 4, length, width), BF16),
-            pltpu.VMEM((2, 3, length, width), BF16),
+            pltpu.VMEM((2, 4, length, width), BF16),
             pltpu.VMEM((length, width), F32),
             pltpu.VMEM((8, width), F32),
             pltpu.VMEM((8, 1, lanes), F32),
@@ -1305,7 +1381,7 @@
             pltpu.VMEM((3, 1, lanes), F32),
             dma((14,)), dma((4,)),
             dma((4, 2)), dma((4, 2)), dma((4,)), dma((4,)),
-            dma((2, 4)), dma((2, 4)), dma((2, 3)), dma((2, 3)),
+            dma((2, 4)), dma((2, 4)), dma((2, 3)), dma((2, 4)),
             dma((8, 4)), dma((8, 4)), dma((4, 3)), dma((4, 3)),
             dma((7,)), dma((7,)), dma((3,)), dma((3,)), dma((7,)),
         ],

time: 371 us -> 312 us (0.84)
  Pallas kernels: 348 us -> 287 us
    pallas_call x1, Pallas kernels: 158 us -> 127 us  [forward(): pl.pallas_call(forward_kernel, out_shape=(struct((8, length, width), BF16...]
    pallas_call x1, Pallas kernels: 191 us -> 160 us  [backward(): pl.pallas_call(backward_kernel, out_shape=(struct((length, width), F32),...]
where the time goes in v1:
time: 312 us; the launch traced here: 309 us
  Pallas kernels  287 us (92%)
  other arithmetic  18.6 us (6%)
    pallas_call x1, Pallas kernels, backward(): pl.pallas_call(backward_kernel, out_shape=(struct((length, width), F32),...  160 us
    pallas_call x1, Pallas kernels, forward(): pl.pallas_call(forward_kernel, out_shape=(struct((8, length, width), BF16...  127 us
    convert_element_type x1, other arithmetic, tensor_parallel(): full_two.astype(F32)  6.73 us

profile of v1, /device:TPU:29, one launch (start us, length us, event | category | flops | bytes accessed | tf_op | source)
XLA Modules:
  0.0 308.6 jit_solution(9981731290001318745)
XLA Ops:
  0.6 127.0 %forward.1 = (bf16[8,128,2048]{2,1,0:T(8,128)(2,1)}, bf16[1024,2048]{1,0:T(8,128)(2,1)}, bf16[2048,768]{1,0:T(8,128)(2,1)}, bf16[2048,1024]{1,0:T(8,128)(2,1)}, ...) custom-call(bf16[128,2048]{1,0:T(8,128)(2,1)} %tok.1, ...), custom_call_target="tpu_custom_call" | custom-call | tf_op jit(solution)/shard_map/forward/pallas_call | solution.py:743
  127.6 159.9 %backward.1 = (f32[128,2048]{1,0:T(8,128)}, f32[128,2048]{1,0:T(8,128)}, bf16[256,6144]{1,0:T(8,128)(2,1)}, bf16[256,8192]{1,0:T(8,128)(2,1)}, bf16[256,2048]{1,...) custom-call(bf16[1024,2048]{1,0:T(8,128)(2,1)} %bitcast.8, ...), custom_call_target="tpu_custom_call" | custom-call | tf_op jit(solution)/shard_map/backward/pallas_call | solution.py:1342
  287.5 0.0 copy-start.1
  287.6 6.7 %convert_element_type.30 = f32[256,8192]{1,0:T(8,128)} convert(bf16[256,8192]{1,0:T(8,128)(2,1)} %get-tuple-element.62) | non-fusion elementwise | flops 2097152 | bytes 12582912 | tf_op jit(solution)/shard_map/convert_element_type | solution.py:1456
  294.3 0.0 copy-done.1
  294.3 0.0 copy-start.3
  294.3 4.4 %convert_element_type.31 = f32[1024,2048]{1,0:T(8,128)} convert(bf16[1024,2048]{1,0:T(8,128)(2,1)S(1)} %copy-done.1) | non-fusion elementwise | flops 2097152 | bytes 12582912 | tf_op jit(solution)/shard_map/convert_element_type | solution.py:1458
  298.7 0.0 copy-done.3
  298.7 0.0 copy-start.5
  298.7 0.0 copy-start
  298.7 3.4 %convert_element_type.28 = f32[256,6144]{1,0:T(8,128)} convert(bf16[256,6144]{1,0:T(8,128)(2,1)S(1)} %copy-done.3) | non-fusion elementwise | flops 1572864 | bytes 9437184 | tf_op jit(solution)/shard_map/convert_element_type | solution.py:1450
  302.2 0.0 copy-start.2
  302.2 0.0 copy-start.4
  302.2 0.0 copy-start.6
  302.2 0.0 copy-start.8
  302.2 0.0 copy-done.5
  302.2 1.6 convert_element_type.29
  303.8 0.0 copy-start.7
  303.8 0.0 copy-done
  303.8 0.2 convert_reduce_fusion
  303.9 0.3 fusion.9
  304.2 0.0 copy-done.2
  304.2 0.3 fusion.12
  304.6 0.0 copy-done.4
  304.6 0.0 copy-done.6
  304.6 0.0 copy-done.8
  304.6 1.6 fusion.8
  306.2 0.0 copy-done.7
  306.2 0.6 fusion.13
  306.8 0.0 copy-start.9
  306.8 0.6 slice.55
  307.4 0.6 slice_reduce_fusion
  308.0 0.6 copy.31
  308.6 0.0 copy-done.9
  (3 shorter events, 0.0 us)
Async XLA Ops:
  287.5 6.7 %copy-start.1 = (bf16[1024,2048]{1,0:T(8,128)(2,1)S(1)}, bf16[1024,2048]{1,0:T(8,128)(2,1)}, u32[]{:S(2)}) copy-start(bf16[1024,2048]{1,0:T(8,128)(2,1)} %get-tuple-element.63) | copy-start | bytes 12582916
  294.3 4.5 %copy-start.3 = (bf16[256,6144]{1,0:T(8,128)(2,1)S(1)}, bf16[256,6144]{1,0:T(8,128)(2,1)}, u32[]{:S(2)}) copy-start(bf16[256,6144]{1,0:T(8,128)(2,1)} %get-tuple-element.60) | copy-start | bytes 9437188
  298.7 3.5 %copy-start.5 = (bf16[256,2048]{1,0:T(8,128)(2,1)S(1)}, bf16[256,2048]{1,0:T(8,128)(2,1)}, u32[]{:S(2)}) copy-start(bf16[256,2048]{1,0:T(8,128)(2,1)} %get-tuple-element.61) | copy-start | bytes 3145732
  298.7 5.0 %copy-start = (bf16[128,2048]{1,0:T(8,128)(2,1)S(1)}, bf16[128,2048]{1,0:T(8,128)(2,1)}, u32[]{:S(2)}) copy-start(bf16[128,2048]{1,0:T(8,128)(2,1)} %tok.1) | copy-start | bytes 1572868
  302.2 2.1 copy-start.2
  302.2 2.4 copy-start.4
  302.2 2.5 copy-start.6
  302.2 2.5 copy-start.8
  303.8 2.5 copy-start.7
  306.8 1.8 copy-start.9

commit v2 on v1

--- a/solution.py
+++ b/solution.py
@@ -333,13 +333,15 @@
         + [(twin, me), (across, me)]
     )
 
-    def along(which, array, gathered, direction, step):
+    def along(which, direction, step):
+        array, gathered, part = pairs[which]
         owner = line - direction * (step - 1)
-        source = array if step == 1 else gathered.at[owner * 2 + col]
+        there = gathered.at[owner * 2 + col, part, :]
+        source = array.at[part, :] if step == 1 else there
         lane = which * 6 + (0 if direction == 1 else 3) + step - 1
         return remote(
             source,
-            gathered.at[owner * 2 + col],
+            there,
             line_send.at[lane],
             line_recv.at[lane],
             (rep, (line + direction) * 2 + col),
@@ -355,74 +357,79 @@
             return line >= step
         return line <= 3 - step
 
-    def sideways(which, array, gathered, direction, step):
+    def sideways(which, direction, step):
+        array, gathered, part = pairs[which]
         owner = line - direction * step
-        source = array if step == 0 else gathered.at[owner * 2 + col]
+        there = gathered.at[owner * 2 + col, part, :]
+        source = array.at[part, :] if step == 0 else there
         lane = which * 7 + (0 if direction == 1 else 3) + step
         return remote(
             source,
-            gathered.at[owner * 2 + col],
+            there,
             col_send.at[lane],
             col_recv.at[lane],
             (rep, other),
         )
 
-    def from_other(which, gathered, direction, step):
+    def from_other(which, direction, step):
+        _, gathered, part = pairs[which]
         owner = line - direction * step
         lane = which * 7 + (0 if direction == 1 else 3) + step
-        here = gathered.at[owner * 2 + 1 - col]
+        here = gathered.at[owner * 2 + 1 - col, part, :]
         return remote(here, here, col_send.at[lane], col_recv.at[lane], (rep, other))
 
-    pairs = ((tok, tok_all), (cot, cot_all))
+    halves = (pl.ds(0, length // 2), pl.ds(length // 2, length // 2))
+    pairs = [
+        (array, gathered, part)
+        for array, gathered in ((tok, tok_all), (cot, cot_all))
+        for part in halves
+    ]
     turns = [(direction, step) for step in (1, 2, 3) for direction in (1, -1)]
 
     def begin(which):
-        array, gathered = pairs[which]
         for direction in (1, -1):
             @pl.when(sends(direction, 1))
             def _(direction=direction):
-                along(which, array, gathered, direction, 1).start()
-        sideways(which, array, gathered, 1, 0).start()
+                along(which, direction, 1).start()
+        sideways(which, 1, 0).start()
 
     def pass_on(which, direction, step):
-        array, gathered = pairs[which]
+        _, gathered, part = pairs[which]
 
         @pl.when(gets(direction, step))
         def _():
             owner = line - direction * step
             lane = which * 6 + (0 if direction == 1 else 3) + step - 1
-            here = gathered.at[owner * 2 + col]
+            here = gathered.at[owner * 2 + col, part, :]
             remote(
                 here, here, line_send.at[lane], line_recv.at[lane], (rep, other)
             ).wait_recv()
-            sideways(which, array, gathered, direction, step).start()
+            sideways(which, direction, step).start()
 
         if step < 3:
             @pl.when(sends(direction, step + 1))
             def _():
-                along(which, array, gathered, direction, step + 1).start()
+                along(which, direction, step + 1).start()
 
     def landed(which):
-        gathered = pairs[which][1]
         for direction, step in turns:
             @pl.when(gets(direction, step))
             def _(direction=direction, step=step):
-                from_other(which, gathered, direction, step).wait_recv()
-
-        from_other(which, gathered, 1, 0).wait_recv()
+                from_other(which, direction, step).wait_recv()
+
+        from_other(which, 1, 0).wait_recv()
 
     def sent(which):
-        array, gathered = pairs[which]
         for direction, step in turns:
             @pl.when(sends(direction, step))
             def _(direction=direction, step=step):
-                along(which, array, gathered, direction, step).wait_send()
+                along(which, direction, step).wait_send()
 
             @pl.when(gets(direction, step))
             def _(direction=direction, step=step):
-                sideways(which, array, gathered, direction, step).wait_send()
-
-        sideways(which, array, gathered, 1, 0).wait_send()
+                sideways(which, direction, step).wait_send()
+
+        sideways(which, 1, 0).wait_send()
 
     mine = pl.multiple_of(rep * share, share)
 
@@ -663,33 +670,48 @@
         )
 
     begin(0)
+    begin(1)
     send_small()
     load_own()
     pass_on(0, 1, 1)
     pass_on(0, -1, 1)
-    send_pieces(1,7,2,6)
+    send_pieces(1,7)
+    pass_on(1, 1, 1)
+    pass_on(1, -1, 1)
+    send_pieces(2,6)
     pass_on(0, 1, 2)
     pass_on(0, -1, 2)
+    pass_on(1, 1, 2)
+    pass_on(1, -1, 2)
     send_pieces(3,5,4)
     pass_on(0, 1, 3)
     pass_on(0, -1, 3)
+    pass_on(1, 1, 3)
+    pass_on(1, -1, 3)
     relay(1,7)
-    begin(1)
+    begin(2)
+    begin(3)
     take_small()
     own[0].wait()
-    relay(2,6)
+    relay(2,6,3,5,4)
     landed(0)
+    landed(1)
     norm_all()
-    relay(3,5,4)
-    pass_on(1, 1, 1)
-    pass_on(1, -1, 1)
+    pass_on(2, 1, 1)
+    pass_on(2, -1, 1)
+    pass_on(3, 1, 1)
+    pass_on(3, -1, 1)
     relay_across(1,7,2,6,3,5,4)
-    pass_on(1, 1, 2)
-    pass_on(1, -1, 2)
+    pass_on(2, 1, 2)
+    pass_on(2, -1, 2)
+    pass_on(3, 1, 2)
+    pass_on(3, -1, 2)
     take_weights()
     project(0)
-    pass_on(1, 1, 3)
-    pass_on(1, -1, 3)
+    pass_on(2, 1, 3)
+    pass_on(2, -1, 3)
+    pass_on(3, 1, 3)
+    pass_on(3, -1, 3)
     attend(0)
     attend(1)
     finish(0)
@@ -707,6 +729,7 @@
     finish(3)
     save_all()
     sent(0)
+    sent(1)
     for step in range(1, 8):
         for copy in pieces(step):
             copy.wait_send()
@@ -720,8 +743,10 @@
     own[1].wait()
     for copy in saves:
         copy.wait()
-    sent(1)
-    landed(1)
+    sent(2)
+    sent(3)
+    landed(2)
+    landed(3)
 
 
 def forward(tok, cot, wide_one, wide_two, mix, narrow, vectors):
@@ -770,7 +795,7 @@
             pltpu.VMEM((1, packed), F32),
             pltpu.VMEM((8, 1, packed), F32),
             pltpu.VMEM((8, width), F32),
-            dma((12,)), dma((12,)), dma((14,)), dma((14,)),
+            dma((24,)), dma((24,)), dma((28,)), dma((28,)),
             dma((7,)), dma((7, 4)), dma((7, 4)),
             dma((1, 7, 2)), dma((1, 7, 2)), dma((2, 7, 2)), dma((2, 7, 2)),
             dma((7,)), dma((7,)), dma((2,)), dma((15,)),
@@ -1395,6 +1420,62 @@
     )
 
 
+def finish_kernel(
+    tok, cot, out_sum, in_sum, out_bias, one, two, mix, narrow, sums,
+    output, input_grad, one_out, two_out, mix_out, narrow_out, narrow_sum, *vectors,
+):
+    own = tok[...].astype(F32)
+    center = own - jnp.mean(own, axis=-1, keepdims=True)
+    scale = lax.rsqrt(jnp.mean(center * center, axis=-1, keepdims=True) + 1e-05)
+    norm = center * scale
+    output[...] = (own + out_sum[...] + out_bias[...]).astype(BF16)
+    pull = in_sum[...]
+    inner = jnp.mean(pull * norm, axis=-1, keepdims=True)
+    pull = scale * (pull - jnp.mean(pull, axis=-1, keepdims=True) - norm * inner)
+    input_grad[...] = (cot[...].astype(F32) + pull).astype(BF16)
+    for source, target in (
+        (one, one_out), (two, two_out), (mix, mix_out), (narrow, narrow_out)
+    ):
+        target[...] = source[...].astype(F32)
+
+    @pl.when(pl.program_id(0) == 0)
+    def _():
+        start = 0
+        for target in vectors:
+            count = target.shape[0]
+            target[...] = sums[0, start : start + count]
+            start += count
+        narrow_sum[...] = vectors[5][...]
+
+
+def finish(tok, cot, out_sum, in_sum, out_bias, one, two, mix, narrow, sums, counts):
+    struct = jax.ShapeDtypeStruct
+    steps = 8
+
+    def rows(array):
+        return pl.BlockSpec((array.shape[0] // steps, array.shape[1]), lambda i: (i, 0))
+
+    def fixed(array):
+        return pl.BlockSpec(array.shape, lambda i: (0, 0))
+
+    moved = (one, two, mix, narrow)
+    return pl.pallas_call(
+        finish_kernel,
+        grid=(steps,),
+        out_shape=(struct(tok.shape, BF16), struct(tok.shape, BF16))
+        + tuple(struct(m.shape, F32) for m in moved)
+        + tuple(struct((count,), F32) for count in (counts[5], *counts)),
+        in_specs=[rows(tok), rows(cot), rows(out_sum), rows(in_sum), fixed(out_bias)]
+        + [rows(m) for m in moved]
+        + [fixed(sums)],
+        out_specs=(rows(tok), rows(tok))
+        + tuple(rows(m) for m in moved)
+        + tuple(pl.BlockSpec((count,), lambda i: (0,)) for count in (counts[5], *counts)),
+        compiler_params=pltpu.CompilerParams(vmem_limit_bytes=60 << 20),
+        name="finish",
+    )(tok, cot, out_sum, in_sum, out_bias, *moved, sums)
+
+
 def tensor_parallel(
     tokens,
     segment_ids,
@@ -1428,35 +1509,31 @@
         narrow_weight, (query, keys, values, probs), context, active, slope, cosine, sine,
         out_part, table,
     )
-    own = tokens.astype(F32)
-    own_center = own - jnp.mean(own, axis=-1, keepdims=True)
-    own_scale = lax.rsqrt(
-        jnp.mean(own_center * own_center, axis=-1, keepdims=True) + 1e-05
-    )
-    own_norm = own_center * own_scale
-    output = (own + out_sum + out_bias).astype(BF16)
-    pulled = own_scale * (
-        in_sum
-        - jnp.mean(in_sum, axis=-1, keepdims=True)
-        - own_norm * jnp.mean(in_sum * own_norm, axis=-1, keepdims=True)
-    )
-    input_grad = (cotangent.astype(F32) + pulled).astype(BF16)
-    flat = sums.reshape(-1)
+    width = D // 8
+    (
+        output, input_grad, grad_one, grad_two, grad_mix, grad_narrow, sum_narrow,
+        sum_first_gain, sum_first_shift, sum_second_gain, sum_second_shift,
+        sum_project, sum_cot, sum_widen,
+    ) = finish(
+        tokens, cotangent, out_sum, in_sum, out_bias, full_one, full_two, full_mix,
+        full_narrow, sums,
+        (width, width, width, width, project_bias.shape[0], width, widen_bias.shape[0]),
+    )
     return (
         output,
         input_grad,
-        flat[:256],
-        flat[256:512],
-        full_one.astype(F32),
-        flat[1024:1792],
-        full_mix.astype(F32),
-        flat[1792:2048],
-        flat[512:768],
-        flat[768:1024],
-        full_two.astype(F32),
-        flat[2048:3072],
-        full_narrow.astype(F32),
-        flat[1792:2048],
+        sum_first_gain,
+        sum_first_shift,
+        grad_one,
+        sum_project,
+        grad_mix,
+        sum_cot,
+        sum_second_gain,
+        sum_second_shift,
+        grad_two,
+        sum_widen,
+        grad_narrow,
+        sum_narrow,
     )
 
 

time: 312 us -> 303 us (0.971)
  other arithmetic: 18.6 us -> 0 us
  Pallas kernels: 287 us -> 298 us
    convert_element_type x5 -> x0, other arithmetic: 17.8 us -> none  [the longest x1 6.73 us: tensor_parallel(): full_two.astype(F32)]
    pallas_call x0 -> x1, Pallas kernels: none -> 15.8 us  [finish(): pl.pallas_call(finish_kernel, grid=(steps,), out_shape=(struct(tok.shape,...]
    pallas_call x1, Pallas kernels: 127 us -> 121 us  [forward(): pl.pallas_call(forward_kernel, out_shape=(struct((8, length, width), BF16...]
where the time goes in v2:
time: 303 us; the launch traced here: 299 us
  Pallas kernels  298 us (98%)
    pallas_call x1, Pallas kernels, backward(): pl.pallas_call(backward_kernel, out_shape=(struct((length, width), F32),...  161 us
    pallas_call x1, Pallas kernels, forward(): pl.pallas_call(forward_kernel, out_shape=(struct((8, length, width), BF16...  121 us
    pallas_call x1, Pallas kernels, finish(): pl.pallas_call(finish_kernel, grid=(steps,), out_shape=(struct(tok.shape,...  15.8 us

profile of v2, /device:TPU:29, one launch (start us, length us, event | category | flops | bytes accessed | tf_op | source)
XLA Modules:
  0.0 298.6 jit_solution(14180944167074641436)
XLA Ops:
  0.6 121.0 %forward.1 = (bf16[8,128,2048]{2,1,0:T(8,128)(2,1)}, bf16[1024,2048]{1,0:T(8,128)(2,1)}, bf16[2048,768]{1,0:T(8,128)(2,1)}, bf16[2048,1024]{1,0:T(8,128)(2,1)}, ...) custom-call(bf16[128,2048]{1,0:T(8,128)(2,1)} %tok.3, ...), custom_call_target="tpu_custom_call" | custom-call | tf_op jit(solution)/shard_map/forward/pallas_call | solution.py:768
  121.7 161.0 %backward.1 = (f32[128,2048]{1,0:T(8,128)}, f32[128,2048]{1,0:T(8,128)}, bf16[256,6144]{1,0:T(8,128)(2,1)}, bf16[256,8192]{1,0:T(8,128)(2,1)}, bf16[256,2048]{1,...) custom-call(bf16[1024,2048]{1,0:T(8,128)(2,1)} %bitcast.1, ...), custom_call_target="tpu_custom_call" | custom-call | tf_op jit(solution)/shard_map/backward/pallas_call | solution.py:1367
  282.7 15.8 %finish.1 = (bf16[128,2048]{1,0:T(8,128)(2,1)}, bf16[128,2048]{1,0:T(8,128)(2,1)}, f32[256,6144]{1,0:T(8,128)}, f32[256,8192]{1,0:T(8,128)}, f32[256,2048]{1,0:T...) custom-call(bf16[128,2048]{1,0:T(8,128)(2,1)} %tok.3, ...), custom_call_target="tpu_custom_call" | custom-call | tf_op jit(solution)/shard_map/finish/pallas_call | solution.py:1462

commit v3 on v2

--- a/solution.py
+++ b/solution.py
@@ -925,22 +925,6 @@
     active, slope = duo.at[pl.ds(0, tokens), :], duo.at[pl.ds(tokens, tokens), :]
     got_cot = load(cot_all, cot, 0)
     got_active = load(active_all, active, 1)
-    got_context = load(context_all, context, 2)
-    for step in range(4):
-        col_copy(0, step).start()
-    got_narrow = [
-        load(narrow.at[:, pl.ds(0, half)], pair.at[pl.ds(0, two_wide), :], 3),
-        load(narrow.at[:, pl.ds(half, half)], pair.at[pl.ds(two_wide, two_wide), :], 4),
-    ]
-    got_slope = load(slope_all, slope, 5)
-    got_second = load(second, wide, 6)
-    got_mix = load(mix, mix_v, 7)
-    got_heads = [
-        load(query_all, query, 8), load(key_all, key, 9), load(value_all, value, 10),
-        load(probs_all, probs, 11), load(cosine_all, cosine, 12), load(sine_all, sine, 13),
-    ]
-    for step in range(4):
-        own_load(step).start()
     vec[...] = jnp.zeros_like(vec)
     sums[...] = jnp.zeros_like(sums)
 
@@ -1260,13 +1244,29 @@
         hand(index, 0, spot_of(index, across), across, (across, me)).wait_recv()
         hand(index, 2, spot_of(index, across), across, (twin, me)).start()
 
+    for step in range(4):
+        col_copy(0, step).start()
     wait(got_active, got_cot)
+    got_context = load(context_all, context, 2)
+    got_narrow = [
+        load(narrow.at[:, pl.ds(0, half)], pair.at[pl.ds(0, two_wide), :], 3),
+        load(narrow.at[:, pl.ds(half, half)], pair.at[pl.ds(two_wide, two_wide), :], 4),
+    ]
+    got_slope = load(slope_all, slope, 5)
+    got_second = load(second, wide, 6)
+    got_mix = load(mix, mix_v, 7)
+    got_heads = [
+        load(query_all, query, 8), load(key_all, key, 9), load(value_all, value, 10),
+        load(probs_all, probs, 11), load(cosine_all, cosine, 12), load(sine_all, sine, 13),
+    ]
+    for step in range(4):
+        own_load(step).start()
     narrow_grad(0)
     trade(3, 0)
+    narrow_grad(2)
+    across_sum(3)
     narrow_grad(1)
     trade(3, 1)
-    narrow_grad(2)
-    across_sum(3)
     narrow_grad(3)
     wait(got_context)
     mix_grad()
@@ -1277,7 +1277,6 @@
     got_cols = [load(cols_two, pair, 3)]
     across_sum(2)
     wait(got_second)
-    send_along(0, 0)
     wide_grad(0, 8)
     trade(1, 0)
     trade(1, 1)
@@ -1287,7 +1286,7 @@
     through_mix()
     got_norm = load(norm_all, cot, 0)
     across_sum(1)
-    send_along(0, 1)
+    send_along(0, 0)
     attend_back(0, 8)
     wait(got_first)
     project_grad(0, 8)
@@ -1295,9 +1294,10 @@
     trade(0, 1)
     across_sum(0)
     wait(*got_cols, got_norm)
-    send_along(0, 2)
+    send_along(0, 1)
     input_part(0)
     input_part(1)
+    send_along(0, 2)
     input_part(2)
     input_part(3)
     send_sums()

time: 303 us -> 303 us (level)
  no operation moved by 1% of the time
where the time goes in v3:
time: 303 us; the launch traced here: 299 us
  Pallas kernels  299 us (99%)
    pallas_call x1, Pallas kernels, backward(): pl.pallas_call(backward_kernel, out_shape=(struct((length, width), F32),...  162 us
    pallas_call x1, Pallas kernels, forward(): pl.pallas_call(forward_kernel, out_shape=(struct((8, length, width), BF16...  121 us
    pallas_call x1, Pallas kernels, finish(): pl.pallas_call(finish_kernel, grid=(steps,), out_shape=(struct(tok.shape,...  15.8 us

profile of v3, /device:TPU:29, one launch (start us, length us, event | category | flops | bytes accessed | tf_op | source)
XLA Modules:
  0.0 299.4 jit_solution(7602529532322293844)
XLA Ops:
  0.6 121.0 %forward.1 = (bf16[8,128,2048]{2,1,0:T(8,128)(2,1)}, bf16[1024,2048]{1,0:T(8,128)(2,1)}, bf16[2048,768]{1,0:T(8,128)(2,1)}, bf16[2048,1024]{1,0:T(8,128)(2,1)}, ...) custom-call(bf16[128,2048]{1,0:T(8,128)(2,1)} %tok.3, ...), custom_call_target="tpu_custom_call" | custom-call | tf_op jit(solution)/shard_map/forward/pallas_call | solution.py:768
  121.7 161.7 %backward.1 = (f32[128,2048]{1,0:T(8,128)}, f32[128,2048]{1,0:T(8,128)}, bf16[256,6144]{1,0:T(8,128)(2,1)}, bf16[256,8192]{1,0:T(8,128)(2,1)}, bf16[256,2048]{1,...) custom-call(bf16[1024,2048]{1,0:T(8,128)(2,1)} %bitcast.1, ...), custom_call_target="tpu_custom_call" | custom-call | tf_op jit(solution)/shard_map/backward/pallas_call | solution.py:1367
  283.4 15.8 %finish.1 = (bf16[128,2048]{1,0:T(8,128)(2,1)}, bf16[128,2048]{1,0:T(8,128)(2,1)}, f32[256,6144]{1,0:T(8,128)}, f32[256,8192]{1,0:T(8,128)}, f32[256,2048]{1,0:T...) custom-call(bf16[128,2048]{1,0:T(8,128)(2,1)} %tok.3, ...), custom_call_target="tpu_custom_call" | custom-call | tf_op jit(solution)/shard_map/finish/pallas_call | solution.py:1462
